TPU v7x, 128 devices: a whole 4x4x4 slice. The times are simulated.
128 devices in a mesh: row: 32 (over y, x, core), col: 4 (over z).
Axes of the slice: x: 4, y: 4, z: 4, core: 2. Of those that a mesh axis runs over, the one named last changes fastest.
Arguments:
- inverse_blocks: bfloat16 [32, 384, 256, 256], P('row', 'col'), may hold values from -6 to 6
- inverse_rows: int32 [32, 384], P('row', 'col'), may hold values from 0 to 95, as said below
- inverse_cols: int32 [32, 384], P('row', 'col'), may hold values from 0 to 95, as said below
- inverse_count: int32 [32, 4], P('row', 'col'), may hold values from 1 to 96, as said below
- panel_rows: int32 [64], replicated, may hold values from -1 to 95, as said below
- lower_old: bfloat16 [3, 64, 256, 256], P(None, 'row'), may hold values from -0.038085938 to 0.038085938
- lower_new: bfloat16 [3, 3, 256, 256], replicated, may hold values from -0.375 to 0.375
- diag_inverse: float32 [3, 256, 256], replicated, may hold values from -6 to 6
Outputs:
- panel_inverse: bfloat16 [3, 64, 256, 256], P(None, 'row', 'col')
- supernode_inverse: float32 [3, 3, 256, 256], replicated
Inputs may be any that keep to these rules, and one draw needn't show every extreme that they name: `panel_rows`: for each row index r in order, 2 entries: distinct block rows congruent to r modulo the number of row indices, at least one, then -1 in the empty slots; some row index fills all 2 in every draw. `inverse_rows`: on row index r every slot names one of the panel rows of r, padding slots too. `inverse_cols`: on column index c every slot names a block column congruent to c modulo the number of column indices; positions may repeat, and repeated blocks add. `inverse_count`: slots 0 to count - 1 of a device's lists are live, the rest padding; one device reaches 96 in every draw.
All inputs are finite; a program needn't handle non-finite values.
Results may differ from a plain program's by a relative error of at most 0.0045.
Values may be sent and summed in bfloat16 or wider, within the bound.
A program may use at most 128 MiB of HBM per device.

v0:
```python
import jax
import jax.numpy as jnp
from jax import lax
from jax.sharding import PartitionSpec as P

exact_mode = lax.Precision.HIGHEST
group_size = 8


def partner_2(value, axis, distance):
    mask = 2**distance
    pairs = [(source, source ^ mask) for source in range(lax.axis_size(axis))]
    return lax.ppermute(value, axis, pairs)


def sent_to_all(value, axis):
    copies = jnp.broadcast_to(value, (lax.axis_size(axis), *value.shape))
    return lax.all_to_all(copies, axis, split_axis=0, concat_axis=0, tiled=True)


def over_copies(value, axis):
    return sent_to_all(value, axis).sum(axis=0)


def linked(blocks_new, left_node, right_node):
    if left_node == right_node:
        return blocks_new[left_node, left_node]
    if right_node > left_node:
        return blocks_new[right_node, left_node]
    return blocks_new[left_node, right_node].T


def per_device(
    inverse_blocks,
    inverse_rows,
    inverse_cols,
    inverse_count,
    panel_rows,
    lower_old,
    lower_new,
    diag_inverse,
):
    blocks = inverse_blocks[0]
    stored_rows = inverse_rows[0]
    stored_cols = inverse_cols[0]
    stored_count = inverse_count[0, 0]
    supernodes = lower_old.shape[0]
    slot_count = lower_old.shape[1]
    block_width = blocks.shape[-1]
    row_devs = lax.axis_size("row")
    col_devs = lax.axis_size("col")
    row_me = lax.axis_index("row")
    col_me = lax.axis_index("col")
    own_rows = lax.dynamic_slice_in_dim(panel_rows, row_me * slot_count, slot_count)
    holding = lower_old
    for bit_index in range(col_devs.bit_length() - 1):
        partner = partner_2(holding, "row", bit_index)
        differ = row_me >> bit_index & 1 != col_me >> bit_index & 1
        holding = jnp.where(differ, partner, holding)
    for bit_index in range(col_devs.bit_length() - 1, row_devs.bit_length() - 1):
        partner = partner_2(holding, "row", bit_index)
        upper_half = row_me >> bit_index & 1 == 1
        holding = jnp.where(
            upper_half,
            jnp.concatenate([partner, holding], axis=1),
            jnp.concatenate([holding, partner], axis=1),
        )
    candidates = holding
    sources = jnp.arange(row_devs // col_devs, dtype=jnp.int32) * col_devs + col_me
    cand_rows = panel_rows.reshape(row_devs, slot_count)[sources].reshape(-1)
    cand_index = jnp.arange(cand_rows.shape[0], dtype=jnp.int32)

    def accumulate(group_index, running):
        offset = group_index * group_size
        block_part = lax.dynamic_slice_in_dim(blocks, offset, group_size)
        row_part = lax.dynamic_slice_in_dim(stored_rows, offset, group_size)
        col_part = lax.dynamic_slice_in_dim(stored_cols, offset, group_size)
        is_live = offset + jnp.arange(group_size, dtype=jnp.int32) < stored_count
        matches = col_part[:, None] == cand_rows[None, :]
        present = jnp.any(matches, axis=1) & is_live
        position = jnp.sum(jnp.where(matches, cand_index[None, :], 0), axis=1)
        factors = jnp.take(candidates, position, axis=1)
        products = jnp.einsum(
            "kab,skbc->skac", block_part, factors, preferred_element_type=jnp.float32
        )
        target = ((row_part[:, None] == own_rows[None, :]) & present[:, None]).astype(jnp.float32)
        return running + jnp.einsum("ks,tkac->tsac", target, products, precision=exact_mode)

    partial_value = lax.fori_loop(
        0,
        (stored_count + group_size - 1) // group_size,
        accumulate,
        jnp.zeros((supernodes, slot_count, block_width, block_width), jnp.float32),
    )
    share_rows = block_width // col_devs
    base_part = over_copies(partial_value, "col")
    lower_links = lower_new.astype(jnp.float32)
    panels = []
    blocks_new = {}
    for node in range(supernodes):
        running = base_part[node]
        for earlier in range(node):
            running = running + jnp.einsum(
                "sab,bc->sac",
                panels[earlier],
                lower_new[node, earlier],
                preferred_element_type=jnp.float32,
            )
        current = (-running).astype(jnp.bfloat16)
        lower_step = lower_old[node]
        term_list = [
            jnp.einsum(
                "sab,sac->bc", panels[earlier], lower_step, preferred_element_type=jnp.float32
            )
            for earlier in range(node)
        ]
        term_list.append(
            jnp.einsum("sab,sac->bc", lower_step, current, preferred_element_type=jnp.float32)
        )
        summed = lax.psum(jnp.stack(term_list), "row")
        for earlier in range(node):
            crossed = summed[earlier]
            for another in range(node):
                crossed = crossed + jnp.dot(
                    linked(blocks_new, earlier, another),
                    lower_links[node, another],
                    precision=exact_mode,
                )
            blocks_new[node, earlier] = -crossed
        diagonal_block = diag_inverse[node] - summed[node]
        for earlier in range(node):
            diagonal_block = diagonal_block - jnp.dot(
                lower_links[node, earlier].T, blocks_new[node, earlier], precision=exact_mode
            )
        blocks_new[node, node] = diagonal_block
        panels.append(current)
    stacked = jnp.stack(panels)
    panel_inverse = lax.dynamic_slice_in_dim(stacked, col_me * share_rows, share_rows, 2)
    empty_block = jnp.zeros((block_width, block_width), jnp.float32)
    supernode_inverse = jnp.stack(
        [
            jnp.stack(
                [
                    blocks_new[node, earlier] if earlier <= node else empty_block
                    for earlier in range(supernodes)
                ]
            )
            for node in range(supernodes)
        ]
    )
    return (panel_inverse, supernode_inverse)


def solution(mesh):
    placed = (
        P("row", "col", None, None),
        P("row", "col"),
        P("row", "col"),
        P("row", "col"),
        P(),
        P(None, "row", None, None),
        P(),
        P(),
    )
    return jax.shard_map(
        per_device,
        mesh=mesh,
        in_specs=placed,
        out_specs=(P(None, "row", "col", None), P()),
        check_vma=False,
    )
```

profile of v0, /device:TPU:1, one launch (start us, length us, event | category | flops | bytes accessed | tf_op | source)
XLA Modules:
  0.0 649.2 jit_solution(10506331962583379529)
XLA Ops:
  12.3 16.2 %collective-permute-done.1 = bf16[3,2,256,256]{3,2,1,0:T(8,128)(2,1)S(1)} collective-permute-done((bf16[3,2,256,256]{3,2,1,0:T(8,128)(2,1)S(1)}, bf16[3,2,256,256]{3,2,1,0:T(8,128)(2,1)S(1)}, u32[]{:S(2)}, u32[]{:S(2)}) %collective-permute-start.1) | collective-permute-done | bytes 786464 | tf_op jit(solution)/shard_map/ppermute | solution.py:13
  31.5 15.3 %collective-permute-done.2 = bf16[3,2,256,256]{3,2,1,0:T(8,128)(2,1)S(1)} collective-permute-done((bf16[3,2,256,256]{3,2,1,0:T(8,128)(2,1)S(1)}, bf16[3,2,256,256]{3,2,1,0:T(8,128)(2,1)S(1)}, u32[]{:S(2)}, u32[]{:S(2)}) %collective-permute-start.2) | collective-permute-done | bytes 786464 | tf_op jit(solution)/shard_map/ppermute | solution.py:13
  48.5 31.3 %collective-permute-done.3 = bf16[3,4,256,256]{3,2,1,0:T(8,128)(2,1)} collective-permute-done((bf16[3,4,256,256]{3,2,1,0:T(8,128)(2,1)S(1)}, bf16[3,4,256,256]{3,2,1,0:T(8,128)(2,1)}, u32[]{:S(2)}, u32[]{:S(2)}) %collective-permute-start.3) | collective-permute-done | bytes 1572896 | tf_op jit(solution)/shard_map/ppermute | solution.py:13
  87.6 62.5 %collective-permute-done.4 = bf16[3,8,256,256]{3,2,1,0:T(8,128)(2,1)} collective-permute-done((bf16[3,8,256,256]{3,2,1,0:T(8,128)(2,1)S(1)}, bf16[3,8,256,256]{3,2,1,0:T(8,128)(2,1)}, u32[]{:S(2)}, u32[]{:S(2)}) %collective-permute-start.4) | collective-permute-done | bytes 3145760 | tf_op jit(solution)/shard_map/ppermute | solution.py:13
  150.1 7.2 %maximum_select_fusion = bf16[3,16,256,256]{3,2,1,0:T(8,128)(2,1)} fusion(bf16[3,8,256,256]{3,2,1,0:T(8,128)(2,1)S(1)} %maximum_select_fusion.1, bf16[3,8,256,256]{3,2,1,0:T(8,128)(2,1)} %collective-permute-done.4, pred[]{:T(512)S(6)} %eq.37), kind=kLoop, calls=%fused_computation.29 | loop fusion | flops 9437184 | bytes 12582913 | tf_op jit(solution)/shard_map/jit(_where)/select_n | solution.py:63
  158.9 280.0 %while.12 = (s32[]{:T(128)}, f32[3,2,256,256]{3,1,2,0:T(2,128)}, s32[]{:T(128)}, s32[96]{0:T(128)S(1)}, s32[8,2]{1,0:T(8,128)}, /*index=5*/bf16[3,16,256,256]{3,...) while((s32[]{:T(128)}, f32[3,2,256,256]{3,1,2,0:T(2,128)}, ...), condition=%wide.wide.region_3.4_spmd.clone, body=%wide.wide.region_0.3_spmd.clone.sunk | while | flops 845022976 | bytes 51385184 | solution.py:89
  167.8 6.9 %copy.94 = f32[3,8,256,256]{3,1,2,0:T(8,128)} copy(f32[3,8,256,256]{2,3,0,1:T(8,128)} %fusion.112) | data formatting | bytes 12582912 | tf_op jit(solution)/shard_map/while/body/kab,skbc->skac/transpose | solution.py:83
  175.6 7.6 %bitcast_add_fusion.3 = f32[3,2,256,256]{3,1,2,0:T(2,128)S(1)} fusion(f32[3,2,256,256]{3,1,2,0:T(2,128)S(1)} %copy-done, f32[3,8,256,256]{3,1,2,0:T(8,128)} %copy.94, pred[8]{0:T(512)(128)(4,1)S(1)} %compare_and_fusion.7, s32[8]{0:T(128)S(1)} %dynamic_slice.46, s32[2]{0:T(128)S(1)} %get-tuple-element.265), kind=kOutput, calls=%fused_computation.8.clone.clone.1 | convolution fusion | flops 38141984 | bytes 9437232 | tf_op jit(solution)/shard_map/while/body/ks,tkac->tsac/dot_general | solution.py:87
  193.2 6.9 %copy.94 = f32[3,8,256,256]{3,1,2,0:T(8,128)} copy(f32[3,8,256,256]{2,3,0,1:T(8,128)} %fusion.112) | data formatting | bytes 12582912 | tf_op jit(solution)/shard_map/while/body/kab,skbc->skac/transpose | solution.py:83
  201.0 7.6 %bitcast_add_fusion.3 = f32[3,2,256,256]{3,1,2,0:T(2,128)S(1)} fusion(f32[3,2,256,256]{3,1,2,0:T(2,128)S(1)} %copy-done, f32[3,8,256,256]{3,1,2,0:T(8,128)} %copy.94, pred[8]{0:T(512)(128)(4,1)S(1)} %compare_and_fusion.7, s32[8]{0:T(128)S(1)} %dynamic_slice.46, s32[2]{0:T(128)S(1)} %get-tuple-element.265), kind=kOutput, calls=%fused_computation.8.clone.clone.1 | convolution fusion | flops 38141984 | bytes 9437232 | tf_op jit(solution)/shard_map/while/body/ks,tkac->tsac/dot_general | solution.py:87
  213.6 5.1 fusion.112
  218.7 6.9 %copy.94 = f32[3,8,256,256]{3,1,2,0:T(8,128)} copy(f32[3,8,256,256]{2,3,0,1:T(8,128)} %fusion.112) | data formatting | bytes 12582912 | tf_op jit(solution)/shard_map/while/body/kab,skbc->skac/transpose | solution.py:83
  226.5 7.6 %bitcast_add_fusion.3 = f32[3,2,256,256]{3,1,2,0:T(2,128)S(1)} fusion(f32[3,2,256,256]{3,1,2,0:T(2,128)S(1)} %copy-done, f32[3,8,256,256]{3,1,2,0:T(8,128)} %copy.94, pred[8]{0:T(512)(128)(4,1)S(1)} %compare_and_fusion.7, s32[8]{0:T(128)S(1)} %dynamic_slice.46, s32[2]{0:T(128)S(1)} %get-tuple-element.265), kind=kOutput, calls=%fused_computation.8.clone.clone.1 | convolution fusion | flops 38141984 | bytes 9437232 | tf_op jit(solution)/shard_map/while/body/ks,tkac->tsac/dot_general | solution.py:87
  244.1 6.9 %copy.94 = f32[3,8,256,256]{3,1,2,0:T(8,128)} copy(f32[3,8,256,256]{2,3,0,1:T(8,128)} %fusion.112) | data formatting | bytes 12582912 | tf_op jit(solution)/shard_map/while/body/kab,skbc->skac/transpose | solution.py:83
  251.9 7.6 %bitcast_add_fusion.3 = f32[3,2,256,256]{3,1,2,0:T(2,128)S(1)} fusion(f32[3,2,256,256]{3,1,2,0:T(2,128)S(1)} %copy-done, f32[3,8,256,256]{3,1,2,0:T(8,128)} %copy.94, pred[8]{0:T(512)(128)(4,1)S(1)} %compare_and_fusion.7, s32[8]{0:T(128)S(1)} %dynamic_slice.46, s32[2]{0:T(128)S(1)} %get-tuple-element.265), kind=kOutput, calls=%fused_computation.8.clone.clone.1 | convolution fusion | flops 38141984 | bytes 9437232 | tf_op jit(solution)/shard_map/while/body/ks,tkac->tsac/dot_general | solution.py:87
  269.6 6.9 %copy.94 = f32[3,8,256,256]{3,1,2,0:T(8,128)} copy(f32[3,8,256,256]{2,3,0,1:T(8,128)} %fusion.112) | data formatting | bytes 12582912 | tf_op jit(solution)/shard_map/while/body/kab,skbc->skac/transpose | solution.py:83
  277.4 7.6 %bitcast_add_fusion.3 = f32[3,2,256,256]{3,1,2,0:T(2,128)S(1)} fusion(f32[3,2,256,256]{3,1,2,0:T(2,128)S(1)} %copy-done, f32[3,8,256,256]{3,1,2,0:T(8,128)} %copy.94, pred[8]{0:T(512)(128)(4,1)S(1)} %compare_and_fusion.7, s32[8]{0:T(128)S(1)} %dynamic_slice.46, s32[2]{0:T(128)S(1)} %get-tuple-element.265), kind=kOutput, calls=%fused_computation.8.clone.clone.1 | convolution fusion | flops 38141984 | bytes 9437232 | tf_op jit(solution)/shard_map/while/body/ks,tkac->tsac/dot_general | solution.py:87
  289.9 5.1 fusion.112
  295.0 6.9 %copy.94 = f32[3,8,256,256]{3,1,2,0:T(8,128)} copy(f32[3,8,256,256]{2,3,0,1:T(8,128)} %fusion.112) | data formatting | bytes 12582912 | tf_op jit(solution)/shard_map/while/body/kab,skbc->skac/transpose | solution.py:83
  302.8 7.6 %bitcast_add_fusion.3 = f32[3,2,256,256]{3,1,2,0:T(2,128)S(1)} fusion(f32[3,2,256,256]{3,1,2,0:T(2,128)S(1)} %copy-done, f32[3,8,256,256]{3,1,2,0:T(8,128)} %copy.94, pred[8]{0:T(512)(128)(4,1)S(1)} %compare_and_fusion.7, s32[8]{0:T(128)S(1)} %dynamic_slice.46, s32[2]{0:T(128)S(1)} %get-tuple-element.265), kind=kOutput, calls=%fused_computation.8.clone.clone.1 | convolution fusion | flops 38141984 | bytes 9437232 | tf_op jit(solution)/shard_map/while/body/ks,tkac->tsac/dot_general | solution.py:87
  320.5 6.9 %copy.94 = f32[3,8,256,256]{3,1,2,0:T(8,128)} copy(f32[3,8,256,256]{2,3,0,1:T(8,128)} %fusion.112) | data formatting | bytes 12582912 | tf_op jit(solution)/shard_map/while/body/kab,skbc->skac/transpose | solution.py:83
  328.3 7.6 %bitcast_add_fusion.3 = f32[3,2,256,256]{3,1,2,0:T(2,128)S(1)} fusion(f32[3,2,256,256]{3,1,2,0:T(2,128)S(1)} %copy-done, f32[3,8,256,256]{3,1,2,0:T(8,128)} %copy.94, pred[8]{0:T(512)(128)(4,1)S(1)} %compare_and_fusion.7, s32[8]{0:T(128)S(1)} %dynamic_slice.46, s32[2]{0:T(128)S(1)} %get-tuple-element.265), kind=kOutput, calls=%fused_computation.8.clone.clone.1 | convolution fusion | flops 38141984 | bytes 9437232 | tf_op jit(solution)/shard_map/while/body/ks,tkac->tsac/dot_general | solution.py:87
  345.9 6.9 %copy.94 = f32[3,8,256,256]{3,1,2,0:T(8,128)} copy(f32[3,8,256,256]{2,3,0,1:T(8,128)} %fusion.112) | data formatting | bytes 12582912 | tf_op jit(solution)/shard_map/while/body/kab,skbc->skac/transpose | solution.py:83
  353.7 7.6 %bitcast_add_fusion.3 = f32[3,2,256,256]{3,1,2,0:T(2,128)S(1)} fusion(f32[3,2,256,256]{3,1,2,0:T(2,128)S(1)} %copy-done, f32[3,8,256,256]{3,1,2,0:T(8,128)} %copy.94, pred[8]{0:T(512)(128)(4,1)S(1)} %compare_and_fusion.7, s32[8]{0:T(128)S(1)} %dynamic_slice.46, s32[2]{0:T(128)S(1)} %get-tuple-element.265), kind=kOutput, calls=%fused_computation.8.clone.clone.1 | convolution fusion | flops 38141984 | bytes 9437232 | tf_op jit(solution)/shard_map/while/body/ks,tkac->tsac/dot_general | solution.py:87
  371.4 6.9 %copy.94 = f32[3,8,256,256]{3,1,2,0:T(8,128)} copy(f32[3,8,256,256]{2,3,0,1:T(8,128)} %fusion.112) | data formatting | bytes 12582912 | tf_op jit(solution)/shard_map/while/body/kab,skbc->skac/transpose | solution.py:83
  379.2 7.6 %bitcast_add_fusion.3 = f32[3,2,256,256]{3,1,2,0:T(2,128)S(1)} fusion(f32[3,2,256,256]{3,1,2,0:T(2,128)S(1)} %copy-done, f32[3,8,256,256]{3,1,2,0:T(8,128)} %copy.94, pred[8]{0:T(512)(128)(4,1)S(1)} %compare_and_fusion.7, s32[8]{0:T(128)S(1)} %dynamic_slice.46, s32[2]{0:T(128)S(1)} %get-tuple-element.265), kind=kOutput, calls=%fused_computation.8.clone.clone.1 | convolution fusion | flops 38141984 | bytes 9437232 | tf_op jit(solution)/shard_map/while/body/ks,tkac->tsac/dot_general | solution.py:87
  396.8 6.9 %copy.94 = f32[3,8,256,256]{3,1,2,0:T(8,128)} copy(f32[3,8,256,256]{2,3,0,1:T(8,128)} %fusion.112) | data formatting | bytes 12582912 | tf_op jit(solution)/shard_map/while/body/kab,skbc->skac/transpose | solution.py:83
  404.6 7.6 %bitcast_add_fusion.3 = f32[3,2,256,256]{3,1,2,0:T(2,128)S(1)} fusion(f32[3,2,256,256]{3,1,2,0:T(2,128)S(1)} %copy-done, f32[3,8,256,256]{3,1,2,0:T(8,128)} %copy.94, pred[8]{0:T(512)(128)(4,1)S(1)} %compare_and_fusion.7, s32[8]{0:T(128)S(1)} %dynamic_slice.46, s32[2]{0:T(128)S(1)} %get-tuple-element.265), kind=kOutput, calls=%fused_computation.8.clone.clone.1 | convolution fusion | flops 38141984 | bytes 9437232 | tf_op jit(solution)/shard_map/while/body/ks,tkac->tsac/dot_general | solution.py:87
  422.3 6.9 %copy.94 = f32[3,8,256,256]{3,1,2,0:T(8,128)} copy(f32[3,8,256,256]{2,3,0,1:T(8,128)} %fusion.112) | data formatting | bytes 12582912 | tf_op jit(solution)/shard_map/while/body/kab,skbc->skac/transpose | solution.py:83
  430.1 7.6 %bitcast_add_fusion.3 = f32[3,2,256,256]{3,1,2,0:T(2,128)S(1)} fusion(f32[3,2,256,256]{3,1,2,0:T(2,128)S(1)} %copy-done, f32[3,8,256,256]{3,1,2,0:T(8,128)} %copy.94, pred[8]{0:T(512)(128)(4,1)S(1)} %compare_and_fusion.7, s32[8]{0:T(128)S(1)} %dynamic_slice.46, s32[2]{0:T(128)S(1)} %get-tuple-element.265), kind=kOutput, calls=%fused_computation.8.clone.clone.1 | convolution fusion | flops 38141984 | bytes 9437232 | tf_op jit(solution)/shard_map/while/body/ks,tkac->tsac/dot_general | solution.py:87
  441.1 41.4 %all_to_all.5 = f32[4,3,2,256,256]{4,3,2,1,0:T(8,128)} all-to-all(f32[4,3,2,256,256]{4,3,2,1,0:T(8,128)S(1)} %broadcast_in_dim.35), channel_id=1, replica_groups=mesh['row'=32,'col'=4] {'col'}, dimensions={0} | all-to-all | bytes 12582912 | tf_op jit(solution)/shard_map/all_to_all | solution.py:18
  495.3 141.2 %all-reduce.4.cloned.1.call-done = (f32[3,256,256]{1,2,0:T(8,128)}, f32[1,256,256]{1,2,0:T(8,128)}, f32[2,256,256]{1,2,0:T(8,128)}) async-done(((f32[3,256,256]{1,2,0:T(8,128)}, f32[1,256,256]{1,2,0:T(8,128)}, f32[2,256,256]{1,2,0:T(8,128)}), (f32[3,256,256]{1,2,0:T(8,128)}, f32[1,256,256]{1,2,0:T(8,128)}, f32[2,256,256]{1,2,0:T(8,128)})) %all-reduce.4.cloned.1.call-update) | async-done | bytes 1572880 | tf_op jit(solution)/shard_map/psum | solution.py:120
  (225 shorter events, 149.5 us)
Async XLA Ops:
  7.2 629.3 %all-reduce.4.cloned.1.call-start = ((), (), s32[]{:S(2)}) async-start(), calls=%async_computation.1 | async-start | bytes 3145728 | tf_op jit(solution)/shard_map/psum | solution.py:120
  7.2 3.6 collective-permute-start
  10.9 17.6 %collective-permute-start.1 = (bf16[3,2,256,256]{3,2,1,0:T(8,128)(2,1)S(1)}, bf16[3,2,256,256]{3,2,1,0:T(8,128)(2,1)S(1)}, u32[]{:S(2)}, u32[]{:S(2)}) collective-permute-start(bf16[3,2,256,256]{3,2,1,0:T(8,128)(2,1)S(1)} %broadcast_select_fusion), channel_id=1, source_target_pairs={{0,8},{4,12},{8,0},{12,4},{16,24},{20,28},{24,16},{28,20},{32,40},... | collective-permute-start | bytes 2359304 | tf_op jit(solution)/shard_map/ppermute | solution.py:13
  28.6 18.2 %collective-permute-start.2 = (bf16[3,2,256,256]{3,2,1,0:T(8,128)(2,1)S(1)}, bf16[3,2,256,256]{3,2,1,0:T(8,128)(2,1)S(1)}, u32[]{:S(2)}, u32[]{:S(2)}) collective-permute-start(bf16[3,2,256,256]{3,2,1,0:T(8,128)(2,1)S(1)} %broadcast_select_fusion.1), channel_id=1, source_target_pairs={{0,16},{4,20},{8,24},{12,28},{16,0},{20,4},{24,8},{28,12},{32,48},... | collective-permute-start | bytes 2359304 | tf_op jit(solution)/shard_map/ppermute | solution.py:13
  47.1 1.5 copy-start.3
  47.1 32.7 %collective-permute-start.3 = (bf16[3,4,256,256]{3,2,1,0:T(8,128)(2,1)S(1)}, bf16[3,4,256,256]{3,2,1,0:T(8,128)(2,1)}, u32[]{:S(2)}, u32[]{:S(2)}) collective-permute-start(bf16[3,4,256,256]{3,2,1,0:T(8,128)(2,1)S(1)} %maximum_select_fusion.2), channel_id=1, source_target_pairs={{0,32},{4,36},{8,40},{12,44},{16,48},{20,52},{24,56},{28,60},{32,0... | collective-permute-start | bytes 4718600 | tf_op jit(solution)/shard_map/ppermute | solution.py:13
  48.5 38.2 %copy-start.9 = (s32[64]{0:T(128)S(1)}, s32[64]{0:T(128)}, u32[]{:S(2)}) copy-start(s32[64]{0:T(128)} %param.14) | copy-start | bytes 772
  83.0 67.1 %collective-permute-start.4 = (bf16[3,8,256,256]{3,2,1,0:T(8,128)(2,1)S(1)}, bf16[3,8,256,256]{3,2,1,0:T(8,128)(2,1)}, u32[]{:S(2)}, u32[]{:S(2)}) collective-permute-start(bf16[3,8,256,256]{3,2,1,0:T(8,128)(2,1)S(1)} %maximum_select_fusion.1), channel_id=1, source_target_pairs={{0,64},{4,68},{8,72},{12,76},{16,80},{20,84},{24,88},{28,92},{32,9... | collective-permute-start | bytes 9437192 | tf_op jit(solution)/shard_map/ppermute | solution.py:13
  87.5 69.8 %copy-start.8 = (s32[8,2]{1,0:T(8,128)}, s32[8,2]{1,0:T(8,128)S(1)}, u32[]{:S(2)}) copy-start(s32[8,2]{1,0:T(8,128)S(1)} %gather_fusion.1) | copy-start | bytes 196
  157.3 1.6 copy-start.10
  157.3 1.6 copy-start.11
  167.8 7.8 %copy-start = (f32[3,2,256,256]{3,1,2,0:T(2,128)S(1)}, f32[3,2,256,256]{3,1,2,0:T(2,128)}, u32[]{:S(2)}) copy-start(f32[3,2,256,256]{3,1,2,0:T(2,128)} %get-tuple-element.243) | copy-start | bytes 4718596 | tf_op jit(solution)/shard_map/while
  183.2 1.1 copy-start.1
  193.2 7.8 %copy-start = (f32[3,2,256,256]{3,1,2,0:T(2,128)S(1)}, f32[3,2,256,256]{3,1,2,0:T(2,128)}, u32[]{:S(2)}) copy-start(f32[3,2,256,256]{3,1,2,0:T(2,128)} %get-tuple-element.243) | copy-start | bytes 4718596 | tf_op jit(solution)/shard_map/while
  208.6 1.1 copy-start.1
  218.7 7.8 %copy-start = (f32[3,2,256,256]{3,1,2,0:T(2,128)S(1)}, f32[3,2,256,256]{3,1,2,0:T(2,128)}, u32[]{:S(2)}) copy-start(f32[3,2,256,256]{3,1,2,0:T(2,128)} %get-tuple-element.243) | copy-start | bytes 4718596 | tf_op jit(solution)/shard_map/while
  234.1 1.1 copy-start.1
  244.1 7.8 %copy-start = (f32[3,2,256,256]{3,1,2,0:T(2,128)S(1)}, f32[3,2,256,256]{3,1,2,0:T(2,128)}, u32[]{:S(2)}) copy-start(f32[3,2,256,256]{3,1,2,0:T(2,128)} %get-tuple-element.243) | copy-start | bytes 4718596 | tf_op jit(solution)/shard_map/while
  259.5 1.1 copy-start.1
  269.6 7.8 %copy-start = (f32[3,2,256,256]{3,1,2,0:T(2,128)S(1)}, f32[3,2,256,256]{3,1,2,0:T(2,128)}, u32[]{:S(2)}) copy-start(f32[3,2,256,256]{3,1,2,0:T(2,128)} %get-tuple-element.243) | copy-start | bytes 4718596 | tf_op jit(solution)/shard_map/while
  295.0 7.8 %copy-start = (f32[3,2,256,256]{3,1,2,0:T(2,128)S(1)}, f32[3,2,256,256]{3,1,2,0:T(2,128)}, u32[]{:S(2)}) copy-start(f32[3,2,256,256]{3,1,2,0:T(2,128)} %get-tuple-element.243) | copy-start | bytes 4718596 | tf_op jit(solution)/shard_map/while
  310.4 1.1 copy-start.1
  320.5 7.8 %copy-start = (f32[3,2,256,256]{3,1,2,0:T(2,128)S(1)}, f32[3,2,256,256]{3,1,2,0:T(2,128)}, u32[]{:S(2)}) copy-start(f32[3,2,256,256]{3,1,2,0:T(2,128)} %get-tuple-element.243) | copy-start | bytes 4718596 | tf_op jit(solution)/shard_map/while
  345.9 7.8 %copy-start = (f32[3,2,256,256]{3,1,2,0:T(2,128)S(1)}, f32[3,2,256,256]{3,1,2,0:T(2,128)}, u32[]{:S(2)}) copy-start(f32[3,2,256,256]{3,1,2,0:T(2,128)} %get-tuple-element.243) | copy-start | bytes 4718596 | tf_op jit(solution)/shard_map/while
  371.4 7.8 %copy-start = (f32[3,2,256,256]{3,1,2,0:T(2,128)S(1)}, f32[3,2,256,256]{3,1,2,0:T(2,128)}, u32[]{:S(2)}) copy-start(f32[3,2,256,256]{3,1,2,0:T(2,128)} %get-tuple-element.243) | copy-start | bytes 4718596 | tf_op jit(solution)/shard_map/while
  396.8 7.8 %copy-start = (f32[3,2,256,256]{3,1,2,0:T(2,128)S(1)}, f32[3,2,256,256]{3,1,2,0:T(2,128)}, u32[]{:S(2)}) copy-start(f32[3,2,256,256]{3,1,2,0:T(2,128)} %get-tuple-element.243) | copy-start | bytes 4718596 | tf_op jit(solution)/shard_map/while
  422.3 7.8 %copy-start = (f32[3,2,256,256]{3,1,2,0:T(2,128)S(1)}, f32[3,2,256,256]{3,1,2,0:T(2,128)}, u32[]{:S(2)}) copy-start(f32[3,2,256,256]{3,1,2,0:T(2,128)} %get-tuple-element.243) | copy-start | bytes 4718596 | tf_op jit(solution)/shard_map/while
  482.5 3.5 copy-start.2
  492.6 1.4 copy-start.5
  494.3 143.3 %copy-start.4 = (bf16[3,3,256,256]{3,2,1,0:T(8,128)(2,1)S(1)}, bf16[3,3,256,256]{3,2,1,0:T(8,128)(2,1)}, u32[]{:S(2)}) copy-start(bf16[3,3,256,256]{3,2,1,0:T(8,128)(2,1)} %param.16) | copy-start | bytes 3538948
  636.5 1.2 copy-start.7
  636.5 1.5 copy-start.6
  (6 other events, 6.9 us)
Sparse Core Ops, SparseCore 0:
  493.7 142.7 all-reduce.3
where the time goes:
time: 650 us; the launch traced here: 649 us
  waiting for transfers between devices  269 us (41%)
  matrix products  148 us (23%)
  local copies, waits for them, and re-layouts  136 us (21%)
  blocking collectives  41.4 us (6%)
  other arithmetic  29.6 us (5%)
  between operations  15 us (2%)
  starting transfers between devices  10.4 us (2%)
    psum x1, waiting for transfers between devices, per_device(): summed = lax.psum(jnp.stack(term_list), 'row')  141 us
    ppermute x5, waiting for transfers between devices, partner_2(): return lax.ppermute(value, axis, pairs)  127 us
    dot_general x11, matrix products, accumulate(): jnp.einsum('ks,tkac->tsac', target, products, precision=exact_mode)  83.6 us
    transpose x11, local copies, waits for them, and re-layouts, accumulate(): jnp.einsum('kab,skbc->skac', block_part, factors, preferred_element_type=...  75.4 us
    dot_general x11, matrix products, accumulate(): jnp.einsum('kab,skbc->skac', block_part, factors, preferred_element_type=...  56 us
    all_to_all x1, blocking collectives, sent_to_all(): return lax.all_to_all(copies, axis, split_axis=0, concat_axis=0, tiled=True)  41.4 us
    gather x11, local copies, waits for them, and re-layouts, accumulate(): factors = jnp.take(candidates, position, axis=1)  38.9 us
  transfers between devices with their start and end apart: 6, of which 6 were waited for; matrix products, arithmetic and copies ran while one was open for 0% of the time, Pallas kernels for 0%

commit v1 on v0

v1 whole, which is shorter than its diff:
```python
import functools

import jax
import jax.numpy as jnp
from jax import lax
from jax.experimental import pallas as pl
from jax.experimental.pallas import tpu as pltpu
from jax.sharding import PartitionSpec as P

MESH = pl.DeviceIdType.MESH
GROUP = 4
BUNDLES = (3, 2, 1)
F32 = jnp.float32
BF16 = jnp.bfloat16


def slot_lists(rows, cols, count, own_rows, cand_rows):
    kmax = rows.shape[0]
    groups = kmax // GROUP + 1
    slots = jnp.arange(kmax, dtype=jnp.int32)
    matches = cols[:, None] == cand_rows[None, :]
    useful = jnp.any(matches, axis=1) & (slots < count)
    position = jnp.sum(
        jnp.where(matches, jnp.arange(cand_rows.shape[0], dtype=jnp.int32)[None, :], 0), axis=1
    )
    mine = useful[None, :] & (rows[None, :] == own_rows[:, None])
    before = slots[None, :] < slots[:, None]
    rank = jnp.sum((before[None] & mine[:, None, :]).astype(jnp.int32), axis=2)
    first = jnp.sum(mine[0].astype(jnp.int32))
    start = (first + GROUP - 1) // GROUP * GROUP
    place = jnp.where(mine[0], rank[0], jnp.where(mine[1], start + rank[1], -1))
    hit = place[None, :] == jnp.arange(groups * GROUP, dtype=jnp.int32)[:, None]
    slot_at = jnp.where(jnp.any(hit, axis=1), jnp.sum(jnp.where(hit, slots[None, :], 0), axis=1), kmax)
    cand_at = jnp.sum(jnp.where(hit, position[None, :], 0), axis=1)
    is_first = (jnp.arange(groups, dtype=jnp.int32) * GROUP < start).astype(F32)
    return slot_at, cand_at, is_first


def kernel(
    slot_at, cand_at, is_first, low, blocks_hbm, new_hbm, diag_hbm,
    panel_out, super_out,
    blocks, lo0, lo1, lo2, acc0, acc1, acc2, new, diag,
    rs_a, rs_b, rs_p, rs_m, u_all,
    g0, g1, g2, c0, c1, c2, h0, h1, h2, zr0, zr1, zr2, hz0, hz1, hz2,
    xr0, xr1, xr2, hx0, hx1, hx2, yr0, yr1, yr2, f0, f1, f2,
    local_sem, lo_send, lo_recv, rs_send, rs_recv, ar_send, ar_recv,
):
    lo = (lo0, lo1, lo2)
    acc = (acc0, acc1, acc2)
    row = lax.axis_index("row")
    z = lax.axis_index("col")
    y = row // 8
    x = (row // 2) % 4
    k = row % 2
    sib = (y * 8 + x * 2 + (1 - k), z)

    def at(dx=0, dy=0, dz=0):
        return ((y + dy + 4) % 4 * 8 + (x + dx + 4) % 4 * 2 + k, (z + dz + 4) % 4)

    barrier = pltpu.get_barrier_semaphore()
    partners = [sib]
    for d in (1, 2, 3):
        partners += [at(dx=d), at(dy=d), at(dz=d)]
    for dev in partners:
        pl.semaphore_signal(barrier, inc=1, device_id=dev, device_id_type=MESH)

    block_copy = pltpu.make_async_copy(blocks_hbm.at[0], blocks.at[pl.ds(0, 96)], local_sem.at[0])
    new_copy = pltpu.make_async_copy(new_hbm, new, local_sem.at[1])
    diag_copy = pltpu.make_async_copy(diag_hbm, diag, local_sem.at[2])
    block_copy.start()
    new_copy.start()
    diag_copy.start()
    blocks[96] = jnp.zeros((256, 256), BF16)

    src_x = z // 2
    src_k = z % 2
    is_src = x % 2 == src_x
    def piece(half, yy, slot):
        return ((yy + 8) % 4 * 2 + half) * 2 + slot

    own_half = x // 2
    left_half = (x + 3) % 4 // 2
    right_half = (x + 1) % 4 // 2
    far_half = 1 - own_half

    sent = {"src": [], "mid": []}

    def send(role, t, cand, dev):
        n = len([1 for (tt, _) in sent[role] if tt == t])
        sent[role].append((t, n))
        pltpu.make_async_remote_copy(
            lo[t].at[cand], lo[t].at[cand], lo_send.at[t, n], lo_recv.at[t, cand],
            device_id=dev, device_id_type=MESH,
        ).start()

    def arrived(t, cand):
        pltpu.make_async_remote_copy(
            lo[t].at[cand], lo[t].at[cand], lo_send.at[t, 0], lo_recv.at[t, cand],
            device_id=sib, device_id_type=MESH,
        ).wait_recv()

    turn = 1 - 2 * k

    def src_step(t, step):
        wide = t == 1
        if step == 1:
            own = piece(own_half, y, k)
            for dev in (at(dx=1), at(dx=-1), at(dy=1), at(dy=-1)):
                send("src", t, own, dev)
        if step == 2:
            c = piece(own_half, y - turn, k)
            arrived(t, c)
            send("src", t, c, at(dy=turn))
            if wide:
                send("src", t, c, at(dx=1))
                send("src", t, c, at(dx=-1))
            send("src", t, c, sib)
            c = piece(own_half, y + turn, k)
            arrived(t, c)
            if wide:
                send("src", t, c, at(dx=1))
                send("src", t, c, at(dx=-1))
            send("src", t, c, sib)
            c = piece(far_half, y, k)
            arrived(t, c)
            send("src", t, c, sib)
        if step == 3:
            c = piece(own_half, y + 2, k)
            arrived(t, c)
            if wide:
                send("src", t, c, at(dx=1))
                send("src", t, c, at(dx=-1))
            send("src", t, c, sib)
            for d in (1, 3):
                c = piece(far_half, y + d, k)
                arrived(t, c)
                send("src", t, c, sib)
        if step == 4:
            c = piece(far_half, y + 2, k)
            arrived(t, c)
            send("src", t, c, sib)

    def mid_step(t, step):
        wide = t == 1
        for d in {1: (0,), 2: (3, 1), 3: (2,), 4: ()}[step]:
            c = piece(left_half, y + d, k)
            arrived(t, c)
            if not wide and d == 0:
                send("mid", t, c, at(dy=1))
                send("mid", t, c, at(dy=-1))
            if not wide and d == 3:
                send("mid", t, c, at(dy=1))
            if d in (0, 1):
                send("mid", t, c, at(dx=1))
            send("mid", t, c, sib)
            c = piece(right_half, y + d, k)
            arrived(t, c)
            if not wide and d == 0:
                send("mid", t, c, at(dy=1))
                send("mid", t, c, at(dy=-1))
            if not wide and d == 1:
                send("mid", t, c, at(dy=-1))
            if d in (2, 3):
                send("mid", t, c, at(dx=-1))
            send("mid", t, c, sib)

    def gather_steps(*steps):
        @pl.when(is_src)
        def _():
            for t, step in steps:
                src_step(t, step)

        @pl.when(jnp.logical_not(is_src))
        def _():
            for t, step in steps:
                mid_step(t, step)

    def from_sibling(t):
        @pl.when(is_src)
        def _():
            for d in (1, 2, 3):
                arrived(t, piece(own_half, y + d, 1 - k))
            for d in range(4):
                arrived(t, piece(far_half, y + d, 1 - k))

        @pl.when(jnp.logical_not(is_src))
        def _():
            for d in range(4):
                arrived(t, piece(left_half, y + d, 1 - k))
                arrived(t, piece(right_half, y + d, 1 - k))

    def multiply(t):
        acc[t][...] = jnp.zeros((2, 256, 256), F32)

        def body(g, carry):
            left = [blocks[slot_at[g * GROUP + i]] for i in range(GROUP)]
            right = [lo[t][cand_at[g * GROUP + i]] for i in range(GROUP)]
            product = jnp.dot(
                jnp.concatenate(left, axis=1), jnp.concatenate(right, axis=0), preferred_element_type=F32
            )
            weight = is_first[g]
            acc[t][0] += product * weight
            acc[t][1] += product * (1.0 - weight)
            return carry

        lax.fori_loop(0, 96 // GROUP + 1, body, 0)

    def quarter(d):
        return pl.ds(pl.multiple_of((z + d) % 4 * 64, 64), 64)

    def rs_copy(t, n):
        a = acc[t]
        src, dst, dev = (
            (a.at[0, quarter(2)], rs_a.at[t], at(dz=1)),
            (a.at[1, quarter(2)], rs_b.at[t], at(dz=3)),
            (a.at[1, quarter(1)], rs_p.at[t, 1], at(dz=1)),
            (a.at[0, quarter(3)], rs_m.at[t, 0], at(dz=3)),
            (a.at[0, quarter(1)], rs_p.at[t, 0], at(dz=1)),
            (a.at[1, quarter(3)], rs_m.at[t, 1], at(dz=3)),
        )[n]
        return pltpu.make_async_remote_copy(
            src, dst, rs_send.at[t, n], rs_recv.at[t, n], device_id=dev, device_id_type=MESH
        )

    def rs_first(t):
        for n in range(4):
            rs_copy(t, n).start()

    def rs_second(t):
        rs_copy(t, 0).wait_recv()
        acc[t][0, quarter(1)] += rs_a[t]
        rs_copy(t, 4).start()
        rs_copy(t, 1).wait_recv()
        acc[t][1, quarter(3)] += rs_b[t]
        rs_copy(t, 5).start()

    def rs_third(t):
        for n in (2, 3, 4, 5):
            rs_copy(t, n).wait_recv()
        return (acc[t][:, quarter(0)] + (rs_p[t] + rs_m[t])).reshape(128, 256)

    def low_rows(t):
        return low[t, :, pl.ds(pl.multiple_of(z * 64, 64), 64), :].reshape(128, 256)

    def across(left, right):
        return lax.dot_general(left, right, (((0,), (0,)), ((), ())), preferred_element_type=F32)

    g = (g0, g1, g2)

    def panel(t):
        running = rs_third(t)
        for e in range(t):
            running = running + jnp.dot(u_all[e], new[t, e], preferred_element_type=F32)
        current = (-running).astype(BF16)
        u_all[t] = current
        panel_out[t] = current.reshape(2, 64, 256)
        if t == 0:
            g0[0] = across(current, low_rows(1))
            g0[1] = across(current, low_rows(2))
            g0[2] = across(low_rows(0), current)
        elif t == 1:
            g1[0] = across(current, low_rows(2))
            g1[1] = across(low_rows(1), current)
        else:
            g2[0] = across(low_rows(2), current)

    def ar(b, phase):
        nb = BUNDLES[b]
        gb, cb, hb, zb, hzb, xb, hxb, yb, fb = (
            (g0, c0, h0, zr0, hz0, xr0, hx0, yr0, f0),
            (g1, c1, h1, zr1, hz1, xr1, hx1, yr1, f1),
            (g2, c2, h2, zr2, hz2, xr2, hx2, yr2, f2),
        )[b]

        def ds(start, size):
            return pl.ds(pl.multiple_of(start, size), size)

        def copy(n, src, dst, dev):
            return pltpu.make_async_remote_copy(
                src, dst, ar_send.at[b, n], ar_recv.at[b, n], device_id=dev, device_id_type=MESH
            )

        def core():
            return [copy(0, gb.at[:, ds(128 * (1 - k), 128)], cb, sib)]

        def over_z():
            return [
                copy(d, hb.at[:, ds((z + d) % 4 * 32, 32)], zb.at[d - 1], at(dz=d)) for d in (1, 2, 3)
            ]

        def over_x():
            return [
                copy(3 + d, hzb.at[:, ds((x + d) % 4 * 8, 8)], xb.at[d - 1], at(dx=d)) for d in (1, 2, 3)
            ]

        def over_y():
            return [copy(6 + d, hxb, yb.at[y], at(dy=d)) for d in (1, 2, 3)]

        base = 128 * k + 32 * z + 8 * x

        def back_x():
            part = fb.at[:, ds(base, 8)]
            return [copy(9 + d, part, part, at(dx=d)) for d in (1, 2, 3)]

        def back_z():
            part = fb.at[:, ds(128 * k + 32 * z, 32)]
            return [copy(12 + d, part, part, at(dz=d)) for d in (1, 2, 3)]

        def back_core():
            part = fb.at[:, ds(128 * k, 128)]
            return [copy(16, part, part, sib)]

        stages = (core, over_z, over_x, over_y, back_x, back_z, back_core)
        if phase > 0:
            for c in stages[phase - 1]():
                c.wait_recv()
        if phase == 1:
            hb[...] = gb[:, ds(128 * k, 128)] + cb[...]
        if phase == 2:
            hzb[...] = hb[:, ds(32 * z, 32)] + (zb[0] + zb[1] + zb[2])
        if phase == 3:
            hxb[...] = hzb[:, ds(8 * x, 8)] + (xb[0] + xb[1] + xb[2])
            yb[y] = hxb[...]
        if phase == 4:
            fb[:, ds(base, 8)] = (yb[0] + yb[1]) + (yb[2] + yb[3])
        if phase < 7:
            for c in stages[phase]():
                c.start()
        if phase == 7:
            for stage in stages:
                for c in stage():
                    c.wait_send()

    def times(value, factor, turned=False):
        high = value.astype(BF16)
        rest = value - high.astype(F32)
        middle = rest.astype(BF16)
        tail = (rest - middle.astype(F32)).astype(BF16)
        total = None
        for part in (tail, middle, high):
            if turned:
                term = across(factor, part)
            else:
                term = jnp.dot(part, factor, preferred_element_type=F32)
            total = term if total is None else total + term
        return total

    pl.semaphore_wait(barrier, len(partners))

    @pl.when(is_src & (k == src_k))
    def _():
        own = piece(own_half, y, 0)
        for t in range(3):
            for s in range(2):
                lo[t][own + s] = low[t, s]
                pltpu.make_async_remote_copy(
                    lo[t].at[own + s], lo[t].at[own + s], lo_send.at[t, 30 + s], lo_recv.at[t, own + s],
                    device_id=sib, device_id_type=MESH,
                ).start()

    @pl.when(is_src & (k != src_k))
    def _():
        own = piece(own_half, y, 0)
        for t in range(3):
            for s in range(2):
                arrived(t, own + s)

    gather_steps((0, 1), (1, 1))

    @pl.when(is_src)
    def _():
        src_step(2, 1)

    gather_steps((0, 2), (1, 2))

    @pl.when(jnp.logical_not(is_src))
    def _():
        mid_step(2, 1)

    gather_steps((0, 3), (1, 3), (0, 4))
    from_sibling(0)
    block_copy.wait()
    multiply(0)
    rs_first(0)
    gather_steps((2, 2), (1, 4))
    from_sibling(1)
    rs_second(0)
    multiply(1)
    rs_first(1)
    new_copy.wait()
    panel(0)
    ar(0, 0)
    gather_steps((2, 3))
    rs_second(1)
    ar(0, 1)
    gather_steps((2, 4))
    from_sibling(2)
    multiply(2)
    rs_first(2)
    panel(1)
    ar(1, 0)
    ar(0, 2)
    rs_second(2)
    ar(1, 1)
    ar(0, 3)
    panel(2)
    ar(2, 0)
    ar(1, 2)
    ar(0, 4)
    ar(2, 1)
    ar(1, 3)
    ar(0, 5)
    ar(2, 2)
    ar(1, 4)
    ar(0, 6)
    ar(2, 3)
    ar(1, 5)
    ar(0, 7)
    diag_copy.wait()
    y00 = diag[0] - f0[2]
    y10 = -(f0[0] + times(y00, new[1, 0]))
    super_out[0, 0] = y00
    super_out[1, 0] = y10
    ar(2, 4)
    ar(1, 6)
    nothing = jnp.zeros((256, 256), F32)
    super_out[0, 1] = nothing
    super_out[0, 2] = nothing
    super_out[1, 2] = nothing
    y20 = -(f0[1] + (times(y00, new[2, 0]) + times(y10, new[2, 1])))
    super_out[2, 0] = y20
    ar(2, 5)
    ar(1, 7)
    y11 = (diag[1] - f1[1]) - times(y10, new[1, 0], True)
    super_out[1, 1] = y11
    y21 = -(f1[0] + (times(y10.T, new[2, 0]) + times(y11, new[2, 1])))
    super_out[2, 1] = y21
    ar(2, 6)
    rest = diag[2] - (times(y20, new[2, 0], True) + times(y21, new[2, 1], True))
    ar(2, 7)
    super_out[2, 2] = rest - f2[0]

    for t in range(3):
        for n in range(6):
            rs_copy(t, n).wait_send()

    def send_done(t, n):
        pltpu.make_async_remote_copy(
            lo[t].at[0], lo[t].at[0], lo_send.at[t, n], lo_recv.at[t, 0],
            device_id=sib, device_id_type=MESH,
        ).wait_send()

    @pl.when(is_src & (k == src_k))
    def _():
        for t in range(3):
            for s in range(2):
                send_done(t, 30 + s)

    @pl.when(is_src)
    def _():
        for t, n in sent["src"]:
            send_done(t, n)

    @pl.when(jnp.logical_not(is_src))
    def _():
        for t, n in sent["mid"]:
            send_done(t, n)


def per_device(
    inverse_blocks,
    inverse_rows,
    inverse_cols,
    inverse_count,
    panel_rows,
    lower_old,
    lower_new,
    diag_inverse,
):
    row_me = lax.axis_index("row")
    col_me = lax.axis_index("col")
    own_rows = lax.dynamic_slice_in_dim(panel_rows, row_me * 2, 2)
    cand_rows = lax.dynamic_index_in_dim(panel_rows.reshape(8, 4, 2), col_me, 1, False).reshape(16)
    lists = slot_lists(inverse_rows[0], inverse_cols[0], inverse_count[0, 0], own_rows, cand_rows)
    smem = pl.BlockSpec(memory_space=pltpu.SMEM)
    vmem = pl.BlockSpec(memory_space=pltpu.VMEM)
    hbm = pl.BlockSpec(memory_space=pl.ANY)

    def each(*shape):
        return [pltpu.VMEM(tuple(nb if s is None else s for s in shape), F32) for nb in BUNDLES]

    return pl.pallas_call(
        kernel,
        out_shape=(
            jax.ShapeDtypeStruct((3, 2, 64, 256), BF16),
            jax.ShapeDtypeStruct((3, 3, 256, 256), F32),
        ),
        in_specs=[smem, smem, smem, vmem, hbm, hbm, hbm],
        out_specs=(vmem, vmem),
        scratch_shapes=[
            pltpu.VMEM((97, 256, 256), BF16),
            *[pltpu.VMEM((16, 256, 256), BF16)] * 3,
            *[pltpu.VMEM((2, 256, 256), F32)] * 3,
            pltpu.VMEM((3, 3, 256, 256), BF16),
            pltpu.VMEM((3, 256, 256), F32),
            pltpu.VMEM((3, 64, 256), F32),
            pltpu.VMEM((3, 64, 256), F32),
            pltpu.VMEM((3, 2, 64, 256), F32),
            pltpu.VMEM((3, 2, 64, 256), F32),
            pltpu.VMEM((3, 128, 256), BF16),
            *each(None, 256, 256),
            *each(None, 128, 256),
            *each(None, 128, 256),
            *each(3, None, 32, 256),
            *each(None, 32, 256),
            *each(3, None, 8, 256),
            *each(None, 8, 256),
            *each(4, None, 8, 256),
            *each(None, 256, 256),
            pltpu.SemaphoreType.DMA((3,)),
            pltpu.SemaphoreType.DMA((3, 32)),
            pltpu.SemaphoreType.DMA((3, 16)),
            pltpu.SemaphoreType.DMA((3, 6)),
            pltpu.SemaphoreType.DMA((3, 6)),
            pltpu.SemaphoreType.DMA((3, 17)),
            pltpu.SemaphoreType.DMA((3, 17)),
        ],
        compiler_params=pltpu.CompilerParams(
            collective_id=0, has_side_effects=True, vmem_limit_bytes=52 * 2**20
        ),
    )(*lists, lower_old, inverse_blocks, lower_new, diag_inverse)


def solution(mesh):
    placed = (
        P("row", "col", None, None),
        P("row", "col"),
        P("row", "col"),
        P("row", "col"),
        P(),
        P(None, "row", None, None),
        P(),
        P(),
    )
    return jax.shard_map(
        per_device,
        mesh=mesh,
        in_specs=placed,
        out_specs=(P(None, "row", "col", None), P()),
        check_vma=False,
    )
```

time: 650 us -> 115 us (0.18)
  waiting for transfers between devices: 269 us -> 0 us
  matrix products: 148 us -> 0 us
  local copies, waits for them, and re-layouts: 136 us -> 7.76 us
  Pallas kernels: 0 us -> 102 us
  blocking collectives: 41.4 us -> 0 us
  other arithmetic: 29.6 us -> 3.22 us
  between operations: 15 us -> 2.01 us
  starting transfers between devices: 10.4 us -> 0 us
    dot_general x39 -> x0, matrix products: 148 us -> none  [the longest x11 83.6 us: accumulate(): jnp.einsum('ks,tkac->tsac', target, products, precision=exact_mode)]
    psum x1 -> x0, waiting for transfers between devices: 141 us -> none  [per_device(): summed = lax.psum(jnp.stack(term_list), 'row')]
    ppermute x5 -> x0, waiting for transfers between devices: 127 us -> none  [partner_2(): return lax.ppermute(value, axis, pairs)]
    pallas_call x0 -> x1, Pallas kernels: none -> 102 us  [per_device(): pl.pallas_call(kernel, out_shape=(jax.ShapeDtypeStruct((3, 2, 64, 256), B...]
    transpose x11 -> x0, local copies, waits for them, and re-layouts: 75.4 us -> none  [accumulate(): jnp.einsum('kab,skbc->skac', block_part, factors, preferred_element_type=...]
    all_to_all x1 -> x0, blocking collectives: 41.4 us -> none  [sent_to_all(): return lax.all_to_all(copies, axis, split_axis=0, concat_axis=0, tiled=True)]
    gather x12 -> x0, local copies, waits for them, and re-layouts: 39.4 us -> none  [the longest x11 38.9 us: accumulate(): factors = jnp.take(candidates, position, axis=1)]
    while x45 -> x0, local copies, waits for them, and re-layouts: 14.1 us -> none
  transfers between devices with their start and end apart: 6 -> 0, of which waited for: 6 -> 0; matrix products, arithmetic and copies ran while one was open for 0% -> 0% of each run, Pallas kernels for 0% -> 0%
where the time goes in v1:
time: 115 us
  Pallas kernels  102 us (89%)
  local copies, waits for them, and re-layouts  7.76 us (7%)
  other arithmetic  3.22 us (3%)
  between operations  2.01 us (2%)
    pallas_call x1, Pallas kernels, per_device(): pl.pallas_call(kernel, out_shape=(jax.ShapeDtypeStruct((3, 2, 64, 256), B...  102 us
    unnamed x6, local copies, waits for them, and re-layouts  6.16 us

profile of v1, /device:TPU:1, one launch (start us, length us, event | category | flops | bytes accessed | tf_op | source)
XLA Modules:
  0.0 115.1 jit_solution(1538347455166158316)
XLA Ops:
  1.3 0.7 dynamic_slice.8
  2.0 0.8 reshape.66
  2.8 0.1 eq.53
  2.9 0.7 fusion.1
  3.7 0.7 compare_reduce_fusion
  4.4 0.7 compare_and_fusion
  5.1 0.6 fusion.2
  6.4 0.1 convert_reduce_fusion
  6.6 0.1 fusion
  6.7 0.1 select_reduce_fusion
  6.8 0.0 copy-start
  6.8 1.1 copy-done
  8.0 0.0 copy-start.1
  8.0 1.1 copy-done.1
  9.1 102.1 %shard_map.95 = (bf16[3,2,64,256]{3,2,1,0:T(8,128)(2,1)S(1)}, f32[3,3,256,256]{3,2,1,0:T(8,128)}) custom-call(s32[100]{0:T(128)S(1)} %broadcast_select_fusion.slot_at, s32[100]{0:T(128)S(1)} %get-tuple-element.2.cand_at, f32[25]{0:T(128)S(1)} %compare_convert_fusion.is_first, bf16[3,2,256,256]{3,2,1,0:T(8,128)(2,1)S(1)} %copy-done, ...), custom_call_target="tpu_custom_call" | custom-call | tf_op jit(solution)/shard_map/pallas_call | solution.py:492
  111.2 0.7 copy.13
  111.9 3.2 %copy.14 = f32[3,3,256,256]{3,2,1,0:T(8,128)} copy(f32[3,3,256,256]{3,2,1,0:T(8,128)} %get-tuple-element.7) | data formatting | bytes 4718592
  (6 shorter events, 0.1 us)
Async XLA Ops:
  6.8 1.1 copy-start
  8.0 1.1 copy-start.1

commit v2 on v1

v2 whole, which is shorter than its diff:
```python
import functools

import jax
import jax.numpy as jnp
from jax import lax
from jax.experimental import pallas as pl
from jax.experimental.pallas import tpu as pltpu
from jax.sharding import PartitionSpec as P

MESH = pl.DeviceIdType.MESH
GROUP = 4
BUNDLES = (3, 2, 1)
PLANE = tuple((dx, dy) for dy in (1, 3, 0, 2) for dx in (1, 3, 0, 2) if (dx, dy) != (0, 0))
F32 = jnp.float32
BF16 = jnp.bfloat16


def slot_lists(rows, cols, count, panel_rows, row, col):
    kmax = rows.shape[1]
    slot = lax.broadcasted_iota(jnp.int32, (kmax, kmax), 0)
    other = lax.broadcasted_iota(jnp.int32, (kmax, kmax), 1)

    def upright(line):
        return jnp.sum(jnp.where(slot == other, jnp.broadcast_to(line, (kmax, kmax)), 0), axis=1, keepdims=True)

    stored_row, stored_col = upright(rows), upright(cols)
    index = lax.broadcasted_iota(jnp.int32, (kmax, 1), 0)
    live = index < count
    useful = jnp.zeros((kmax, 1), jnp.int32)
    position = jnp.zeros((kmax, 1), jnp.int32)
    for i in range(8):
        for j in range(2):
            same = stored_col == panel_rows[(i * 4 + col) * 2 + j]
            useful = jnp.where(same & live, 1, useful)
            position = jnp.where(same, i * 2 + j, position)
    mine = [jnp.where(stored_row == panel_rows[row * 2 + p], useful, 0) for p in range(2)]
    flat = [jnp.sum(jnp.where(slot == other, jnp.broadcast_to(m, (kmax, kmax)), 0), axis=0, keepdims=True) for m in mine]
    rank = [
        jnp.sum(jnp.where(other < slot, jnp.broadcast_to(f, (kmax, kmax)), 0), axis=1, keepdims=True) for f in flat
    ]
    first = jnp.sum(jnp.broadcast_to(flat[0], (8, kmax)), axis=1, keepdims=True)[0:1]
    padding = jnp.where(first % GROUP == 0, 0, GROUP - first % GROUP)
    start = first + padding
    place = jnp.where(mine[0] == 1, rank[0], jnp.where(mine[1] == 1, start + rank[1], -1))
    hit = place == lax.broadcasted_iota(jnp.int32, (kmax, 128), 1)
    filled = jnp.sum(jnp.where(hit, 1, 0), axis=0, keepdims=True)
    slot_at = jnp.sum(jnp.where(hit, index, 0), axis=0, keepdims=True)
    cand_at = jnp.sum(jnp.where(hit, position, 0), axis=0, keepdims=True)
    lane = lax.broadcasted_iota(jnp.int32, (1, 128), 1)
    is_first = jnp.where(lane * GROUP < start, 1, 0)
    return jnp.where(filled == 1, slot_at, kmax), cand_at, is_first


def kernel(
    rows, cols, count, panel_rows, low, blocks_hbm, new_hbm, diag_hbm,
    panel_out, super_out,
    lists, table,
    blocks, lo0, lo1, lo2, acc0, acc1, acc2, new, diag,
    rs_a, rs_b, rs_p, rs_m, u_all,
    g0, g1, g2, c0, c1, c2, h0, h1, h2, p0, p1, p2, s0, s1, s2, y0, y1, y2, f0, f1, f2,
    local_sem, lo_send, lo_recv, rs_send, rs_recv, ar_send, ar_recv,
):
    lo = (lo0, lo1, lo2)
    acc = (acc0, acc1, acc2)
    row = lax.axis_index("row")
    z = lax.axis_index("col")
    y = row // 8
    x = (row // 2) % 4
    k = row % 2
    sib = (y * 8 + x * 2 + (1 - k), z)

    def at(dx=0, dy=0, dz=0):
        return ((y + dy + 4) % 4 * 8 + (x + dx + 4) % 4 * 2 + k, (z + dz + 4) % 4)

    barrier = pltpu.get_barrier_semaphore()
    partners = [sib]
    partners += [at(dx=dx, dy=dy) for dx, dy in PLANE]
    partners += [at(dz=d) for d in (1, 2, 3)]
    for dev in partners:
        pl.semaphore_signal(barrier, inc=1, device_id=dev, device_id_type=MESH)

    block_copy = pltpu.make_async_copy(blocks_hbm.at[0], blocks.at[pl.ds(0, 96)], local_sem.at[0])
    new_copy = pltpu.make_async_copy(new_hbm, new, local_sem.at[1])
    diag_copy = pltpu.make_async_copy(diag_hbm, diag, local_sem.at[2])
    block_copy.start()
    new_copy.start()
    diag_copy.start()
    blocks[96] = jnp.zeros((256, 256), BF16)

    src_x = z // 2
    src_k = z % 2
    is_src = x % 2 == src_x
    def piece(half, yy, slot):
        return ((yy + 8) % 4 * 2 + half) * 2 + slot

    own_half = x // 2
    left_half = (x + 3) % 4 // 2
    right_half = (x + 1) % 4 // 2
    far_half = 1 - own_half

    sent = {"src": [], "mid": []}

    def send(role, t, cand, dev):
        n = len([1 for (tt, _) in sent[role] if tt == t])
        sent[role].append((t, n))
        pltpu.make_async_remote_copy(
            lo[t].at[cand], lo[t].at[cand], lo_send.at[t, n], lo_recv.at[t, cand],
            device_id=dev, device_id_type=MESH,
        ).start()

    def arrived(t, cand):
        pltpu.make_async_remote_copy(
            lo[t].at[cand], lo[t].at[cand], lo_send.at[t, 0], lo_recv.at[t, cand],
            device_id=sib, device_id_type=MESH,
        ).wait_recv()

    def src_step(t, step):
        if step == 1:
            own = piece(own_half, y, k)
            for dev in (at(dx=1), at(dx=-1), at(dy=1), at(dy=-1), at(dy=2)):
                send("src", t, own, dev)
        if step == 2:
            for d in (1, 3):
                c = piece(own_half, y + d, k)
                arrived(t, c)
                send("src", t, c, sib)
        if step == 3:
            c = piece(own_half, y + 2, k)
            arrived(t, c)
            send("src", t, c, at(dx=1))
            send("src", t, c, at(dx=-1))
            send("src", t, c, sib)
        if step >= 4:
            for d in {4: (0,), 5: (1, 3), 6: (2,)}[step]:
                c = piece(far_half, y + d, k)
                arrived(t, c)
                send("src", t, c, sib)

    def mid_step(t, step):
        for d in {1: (0,), 2: (3, 1), 3: (2,)}[step]:
            c = piece(left_half, y + d, k)
            arrived(t, c)
            if d == 0:
                send("mid", t, c, at(dy=1))
                send("mid", t, c, at(dy=-1))
            if d in (0, 1):
                send("mid", t, c, at(dx=1))
            send("mid", t, c, sib)
            c = piece(right_half, y + d, k)
            arrived(t, c)
            if d == 0:
                send("mid", t, c, at(dy=1))
                send("mid", t, c, at(dy=-1))
            if d in (2, 3):
                send("mid", t, c, at(dx=-1))
            send("mid", t, c, sib)

    def gather_steps(src_steps, mid_steps):
        @pl.when(is_src)
        def _():
            for t, step in src_steps:
                src_step(t, step)

        @pl.when(jnp.logical_not(is_src))
        def _():
            for t, step in mid_steps:
                mid_step(t, step)

    def from_sibling(t):
        @pl.when(is_src)
        def _():
            for d in (1, 2, 3):
                arrived(t, piece(own_half, y + d, 1 - k))
            for d in range(4):
                arrived(t, piece(far_half, y + d, 1 - k))

        @pl.when(jnp.logical_not(is_src))
        def _():
            for d in range(4):
                arrived(t, piece(left_half, y + d, 1 - k))
                arrived(t, piece(right_half, y + d, 1 - k))

    def multiply(t, begin, end):
        if begin == 0:
            acc[t][...] = jnp.zeros((2, 256, 256), F32)

        def body(g, carry):
            left = [blocks[table[0, g * GROUP + i]] for i in range(GROUP)]
            right = [lo[t][table[1, g * GROUP + i]] for i in range(GROUP)]
            product = jnp.dot(
                jnp.concatenate(left, axis=1), jnp.concatenate(right, axis=0), preferred_element_type=F32
            )
            weight = table[2, g].astype(F32)
            acc[t][0] += product * weight
            acc[t][1] += product * (1.0 - weight)
            return carry

        lax.fori_loop(begin, end, body, 0, unroll=5)

    def quarter(d):
        return pl.ds(pl.multiple_of((z + d) % 4 * 64, 64), 64)

    def rs_copy(t, n):
        a = acc[t]
        src, dst, dev = (
            (a.at[0, quarter(2)], rs_a.at[t], at(dz=1)),
            (a.at[1, quarter(2)], rs_b.at[t], at(dz=3)),
            (a.at[1, quarter(1)], rs_p.at[t, 1], at(dz=1)),
            (a.at[0, quarter(3)], rs_m.at[t, 0], at(dz=3)),
            (a.at[0, quarter(1)], rs_p.at[t, 0], at(dz=1)),
            (a.at[1, quarter(3)], rs_m.at[t, 1], at(dz=3)),
        )[n]
        return pltpu.make_async_remote_copy(
            src, dst, rs_send.at[t, n], rs_recv.at[t, n], device_id=dev, device_id_type=MESH
        )

    def rs_first(t):
        for n in range(4):
            rs_copy(t, n).start()

    def rs_second(t):
        rs_copy(t, 0).wait_recv()
        acc[t][0, quarter(1)] += rs_a[t]
        rs_copy(t, 4).start()
        rs_copy(t, 1).wait_recv()
        acc[t][1, quarter(3)] += rs_b[t]
        rs_copy(t, 5).start()

    def rs_third(t):
        for n in (2, 3, 4, 5):
            rs_copy(t, n).wait_recv()
        return (acc[t][:, quarter(0)] + (rs_p[t] + rs_m[t])).reshape(128, 256)

    def low_rows(t):
        return low[t, :, pl.ds(pl.multiple_of(z * 64, 64), 64), :].reshape(128, 256)

    def across(left, right):
        return lax.dot_general(left, right, (((0,), (0,)), ((), ())), preferred_element_type=F32)

    g = (g0, g1, g2)

    def earlier(t):
        total = jnp.dot(u_all[0], new[t, 0], preferred_element_type=F32)
        for e in range(1, t):
            total = total + jnp.dot(u_all[e], new[t, e], preferred_element_type=F32)
        return total

    def panel(t):
        running = rs_third(t)
        if t > 0:
            running = running + earlier(t)
        current = (-running).astype(BF16)
        u_all[t] = current
        panel_out[t] = current.reshape(2, 64, 256)
        if t == 0:
            g0[0] = across(current, low_rows(1))
            g0[1] = across(current, low_rows(2))
            g0[2] = across(low_rows(0), current)
        elif t == 1:
            g1[0] = across(current, low_rows(2))
            g1[1] = across(low_rows(1), current)

    def halves(value):
        high = value.astype(BF16)
        return high, (value - high.astype(F32)).astype(BF16)

    def last_contraction():
        total = None
        for part in halves(earlier(2)):
            term = across(low_rows(2), part)
            total = term if total is None else total + term
        for p in range(2):
            for part in halves(acc2[p]):
                total = total + across(low[2, p], part)
        g2[0] = -total

    def ar(b, phase):
        gb, cb, hb, pb, sb, yb, fb = (
            (g0, c0, h0, p0, s0, y0, f0),
            (g1, c1, h1, p1, s1, y1, f1),
            (g2, c2, h2, p2, s2, y2, f2),
        )[b]

        def ds(start, size):
            return pl.ds(pl.multiple_of(start, size), size)

        def copy(n, src, dst, dev):
            return pltpu.make_async_remote_copy(
                src, dst, ar_send.at[b, n], ar_recv.at[b, n], device_id=dev, device_id_type=MESH
            )

        mine = y * 4 + x
        base = 128 * k + 8 * mine
        peers = [(dx, dy) for dx, dy in PLANE]

        def core():
            return [copy(0, gb.at[:, ds(128 * (1 - k), 128)], cb, sib)]

        def over_plane():
            copies = []
            for dx, dy in peers:
                other = (y + dy) % 4 * 4 + (x + dx) % 4
                copies.append(copy(1, hb.at[:, ds(8 * other, 8)], pb.at[mine], at(dx=dx, dy=dy)))
            return copies

        def over_z():
            return [copy(1 + d, sb, yb.at[z], at(dz=d)) for d in (1, 3, 2)]

        def back_plane():
            part = fb.at[:, ds(base, 8)]
            return [copy(5, part, part, at(dx=dx, dy=dy)) for dx, dy in peers]

        def back_core():
            part = fb.at[:, ds(128 * k, 128)]
            return [copy(6, part, part, sib)]

        def plane_wait():
            return [copy(1, hb.at[:, pl.ds(0, 120)], hb.at[:, pl.ds(0, 120)], sib)]

        def back_wait():
            return [copy(5, fb.at[:, pl.ds(0, 120)], fb.at[:, pl.ds(0, 120)], sib)]

        stages = (core, over_plane, over_z, back_plane, back_core)
        waits = (core, plane_wait, over_z, back_wait, back_core)
        if phase > 0:
            for c in waits[phase - 1]():
                c.wait_recv()
        if phase == 1:
            hb[...] = gb[:, ds(128 * k, 128)] + cb[...]
            pb[mine] = hb[:, ds(8 * mine, 8)]
        if phase == 2:
            total = [pb[i] for i in range(16)]
            while len(total) > 1:
                total = [total[i] + total[i + 1] for i in range(0, len(total), 2)]
            sb[...] = total[0]
            yb[z] = total[0]
        if phase == 3:
            fb[:, ds(base, 8)] = (yb[0] + yb[1]) + (yb[2] + yb[3])
        if phase < 5:
            for c in stages[phase]():
                c.start()
        if phase == 5:
            for stage in waits:
                for c in stage():
                    c.wait_send()

    def times(value, factor, turned=False):
        total = None
        for part in halves(value):
            if turned:
                term = across(factor, part)
            else:
                term = jnp.dot(part, factor, preferred_element_type=F32)
            total = term if total is None else total + term
        return total

    pl.semaphore_wait(barrier, len(partners))

    @pl.when(is_src & (k == src_k))
    def _():
        own = piece(own_half, y, 0)
        for t in range(3):
            for s in range(2):
                lo[t][own + s] = low[t, s]
                pltpu.make_async_remote_copy(
                    lo[t].at[own + s], lo[t].at[own + s], lo_send.at[t, 30 + s], lo_recv.at[t, own + s],
                    device_id=sib, device_id_type=MESH,
                ).start()

    @pl.when(is_src & (k != src_k))
    def _():
        own = piece(own_half, y, 0)
        for t in range(3):
            for s in range(2):
                arrived(t, own + s)

    gather_steps(((0, 1), (1, 1), (2, 1)), ())
    found = slot_lists(rows[...], cols[...], count[0, 0], panel_rows, row, z)
    for i in range(3):
        lists[i : i + 1, :] = found[i]
    table_copy = pltpu.make_async_copy(lists, table, local_sem.at[3])
    table_copy.start()
    gather_steps(((0, 2),), ((0, 1),))
    gather_steps(((1, 2), (0, 3)), ((1, 1),))
    gather_steps(((2, 2), (1, 3), (0, 4)), ((2, 1), (0, 2), (0, 3)))
    gather_steps(((2, 3), (1, 4)), ((1, 2), (1, 3)))
    gather_steps(((0, 5), (0, 6)), ())
    from_sibling(0)
    table_copy.wait()
    block_copy.wait()
    multiply(0, 0, 10)
    gather_steps(((2, 4),), ((2, 2), (2, 3)))
    multiply(0, 10, 25)
    rs_first(0)
    gather_steps(((1, 5), (1, 6)), ())
    from_sibling(1)
    multiply(1, 0, 10)
    rs_second(0)
    gather_steps(((2, 5), (2, 6)), ())
    multiply(1, 10, 25)
    rs_first(1)
    new_copy.wait()
    panel(0)
    ar(0, 0)
    from_sibling(2)
    multiply(2, 0, 10)
    rs_second(1)
    ar(0, 1)
    multiply(2, 10, 25)
    rs_first(2)
    panel(1)
    ar(1, 0)
    last_contraction()
    ar(2, 0)
    ar(1, 1)
    ar(2, 1)
    rs_second(2)
    ar(0, 2)
    panel(2)
    ar(1, 2)
    ar(2, 2)
    ar(0, 3)
    ar(1, 3)
    ar(2, 3)
    ar(0, 4)
    ar(0, 5)
    diag_copy.wait()
    y00 = diag[0] - f0[2]
    y10 = -(f0[0] + times(y00, new[1, 0]))
    super_out[0, 0] = y00
    super_out[1, 0] = y10
    ar(1, 4)
    nothing = jnp.zeros((256, 256), F32)
    super_out[0, 1] = nothing
    super_out[0, 2] = nothing
    super_out[1, 2] = nothing
    y20 = -(f0[1] + (times(y00, new[2, 0]) + times(y10, new[2, 1])))
    super_out[2, 0] = y20
    ar(2, 4)
    ar(1, 5)
    y11 = (diag[1] - f1[1]) - times(y10, new[1, 0], True)
    super_out[1, 1] = y11
    y21 = -(f1[0] + (times(y10.T, new[2, 0]) + times(y11, new[2, 1])))
    super_out[2, 1] = y21
    rest = diag[2] - (times(y20, new[2, 0], True) + times(y21, new[2, 1], True))
    ar(2, 5)
    super_out[2, 2] = rest - f2[0]

    for t in range(3):
        for n in range(6):
            rs_copy(t, n).wait_send()

    def send_done(t, n):
        pltpu.make_async_remote_copy(
            lo[t].at[0], lo[t].at[0], lo_send.at[t, n], lo_recv.at[t, 0],
            device_id=sib, device_id_type=MESH,
        ).wait_send()

    @pl.when(is_src & (k == src_k))
    def _():
        for t in range(3):
            for s in range(2):
                send_done(t, 30 + s)

    @pl.when(is_src)
    def _():
        for t, n in sent["src"]:
            send_done(t, n)

    @pl.when(jnp.logical_not(is_src))
    def _():
        for t, n in sent["mid"]:
            send_done(t, n)


def per_device(
    inverse_blocks,
    inverse_rows,
    inverse_cols,
    inverse_count,
    panel_rows,
    lower_old,
    lower_new,
    diag_inverse,
):
    smem = pl.BlockSpec(memory_space=pltpu.SMEM)
    vmem = pl.BlockSpec(memory_space=pltpu.VMEM)
    hbm = pl.BlockSpec(memory_space=pltpu.HBM)

    def each(*shape):
        return [pltpu.VMEM(tuple(nb if s is None else s for s in shape), F32) for nb in BUNDLES]

    return pl.pallas_call(
        kernel,
        out_shape=(
            jax.ShapeDtypeStruct((3, 2, 64, 256), BF16),
            jax.ShapeDtypeStruct((3, 3, 256, 256), F32),
        ),
        in_specs=[vmem, vmem, smem, smem, vmem, hbm, hbm, hbm],
        out_specs=(vmem, vmem),
        scratch_shapes=[
            pltpu.VMEM((3, 128), jnp.int32),
            pltpu.SMEM((3, 128), jnp.int32),
            pltpu.VMEM((97, 256, 256), BF16),
            *[pltpu.VMEM((16, 256, 256), BF16)] * 3,
            *[pltpu.VMEM((2, 256, 256), F32)] * 3,
            pltpu.VMEM((3, 3, 256, 256), BF16),
            pltpu.VMEM((3, 256, 256), F32),
            pltpu.VMEM((3, 64, 256), F32),
            pltpu.VMEM((3, 64, 256), F32),
            pltpu.VMEM((3, 2, 64, 256), F32),
            pltpu.VMEM((3, 2, 64, 256), F32),
            pltpu.VMEM((3, 128, 256), BF16),
            *each(None, 256, 256),
            *each(None, 128, 256),
            *each(None, 128, 256),
            *each(16, None, 8, 256),
            *each(None, 8, 256),
            *each(4, None, 8, 256),
            *each(None, 256, 256),
            pltpu.SemaphoreType.DMA((4,)),
            pltpu.SemaphoreType.DMA((3, 32)),
            pltpu.SemaphoreType.DMA((3, 16)),
            pltpu.SemaphoreType.DMA((3, 6)),
            pltpu.SemaphoreType.DMA((3, 6)),
            pltpu.SemaphoreType.DMA((3, 7)),
            pltpu.SemaphoreType.DMA((3, 7)),
        ],
        compiler_params=pltpu.CompilerParams(
            collective_id=0, has_side_effects=True, vmem_limit_bytes=52 * 2**20
        ),
    )(inverse_rows, inverse_cols, inverse_count, panel_rows, lower_old, inverse_blocks, lower_new, diag_inverse)


def solution(mesh):
    placed = (
        P("row", "col", None, None),
        P("row", "col"),
        P("row", "col"),
        P("row", "col"),
        P(),
        P(None, "row", None, None),
        P(),
        P(),
    )
    return jax.shard_map(
        per_device,
        mesh=mesh,
        in_specs=placed,
        out_specs=(P(None, "row", "col", None), P()),
        check_vma=False,
    )
```

time: 115 us -> 88.6 us (0.77)
  Pallas kernels: 102 us -> 78.9 us
  other arithmetic: 3.22 us -> 0 us
    pallas_call x1, Pallas kernels: 102 us -> 78.9 us  [per_device(): pl.pallas_call(kernel, out_shape=(jax.ShapeDtypeStruct((3, 2, 64, 256), B...]
    unnamed x6 -> x12, local copies, waits for them, and re-layouts: 6.16 us -> 8.12 us
    reduce_sum x4 -> x0, other arithmetic: 1.6 us -> none  [the longest x1 0.75 us: slot_lists(): jnp.sum(jnp.where(matches, jnp.arange(cand_rows.shape[0], dtype=jnp.int32...]
where the time goes in v2:
time: 88.6 us; the launch traced here: 88.3 us
  Pallas kernels  78.9 us (89%)
  local copies, waits for them, and re-layouts  8.12 us (9%)
  between operations  1.3 us (1%)
    pallas_call x1, Pallas kernels, per_device(): pl.pallas_call(kernel, out_shape=(jax.ShapeDtypeStruct((3, 2, 64, 256), B...  78.9 us
    unnamed x12, local copies, waits for them, and re-layouts  8.12 us

profile of v2, /device:TPU:1, one launch (start us, length us, event | category | flops | bytes accessed | tf_op | source)
XLA Modules:
  0.0 88.3 jit_solution(13931658163931375933)
XLA Ops:
  1.3 0.0 copy-start
  1.3 1.1 %copy-done = bf16[3,2,256,256]{3,2,1,0:T(8,128)(2,1)S(1)} copy-done((bf16[3,2,256,256]{3,2,1,0:T(8,128)(2,1)S(1)}, bf16[3,2,256,256]{3,2,1,0:T(8,128)(2,1)}, u32[]{:S(2)}) %copy-start) | copy-done | bytes 786456
  2.4 0.0 copy-start.1
  2.4 1.1 %copy-done.1 = f32[3,256,256]{2,1,0:T(8,128)S(1)} copy-done((f32[3,256,256]{2,1,0:T(8,128)S(1)}, f32[3,256,256]{2,1,0:T(8,128)}, u32[]{:S(2)}) %copy-start.1) | copy-done | bytes 786456
  3.5 0.0 copy-start.2
  3.5 0.7 copy-done.2
  4.2 0.0 copy-start.3
  4.2 0.7 copy-done.3
  4.9 0.0 copy-start.4
  4.9 0.7 copy-done.4
  5.5 78.9 %shard_map.95 = (bf16[3,2,64,256]{3,2,1,0:T(8,128)(2,1)S(1)}, f32[3,3,256,256]{3,2,1,0:T(8,128)}) custom-call(s32[1,96]{1,0:T(1,128)S(1)} %copy-done.2, s32[1,96]{1,0:T(1,128)S(1)} %copy-done.3, s32[1,1]{1,0:T(1,128)S(6)} %copy.12.count, s32[64]{0:T(128)S(1)} %copy-done.4, bf16[3,2,256,256]{3,2,1,0:T(8,128)(2,1)S(1)} %copy-done, ...), custom_call_target="tpu_custom_call" | custom-call | tf_op jit(solution)/shard_map/pallas_call | solution.py:493
  84.4 0.7 copy.13
  85.1 3.2 %copy.14 = f32[3,3,256,256]{3,2,1,0:T(8,128)} copy(f32[3,3,256,256]{3,2,1,0:T(8,128)} %get-tuple-element.5) | data formatting | bytes 4718592
Async XLA Ops:
  1.3 1.1 %copy-start = (bf16[3,2,256,256]{3,2,1,0:T(8,128)(2,1)S(1)}, bf16[3,2,256,256]{3,2,1,0:T(8,128)(2,1)}, u32[]{:S(2)}) copy-start(bf16[3,2,256,256]{3,2,1,0:T(8,128)(2,1)} %low.1) | copy-start | bytes 2359300
  2.4 1.1 %copy-start.1 = (f32[3,256,256]{2,1,0:T(8,128)S(1)}, f32[3,256,256]{2,1,0:T(8,128)}, u32[]{:S(2)}) copy-start(f32[3,256,256]{2,1,0:T(8,128)} %diag_hbm.1) | copy-start | bytes 2359300
  3.5 0.7 copy-start.2
  4.2 0.7 copy-start.3
  4.9 0.7 copy-start.4

commit v3 on v2

--- a/solution.py
+++ b/solution.py
@@ -52,11 +52,11 @@
 
 
 def kernel(
-    rows, cols, count, panel_rows, low, blocks_hbm, new_hbm, diag_hbm,
+    rows_hbm, cols_hbm, count_hbm, panel_hbm, low_hbm, blocks_hbm, new_hbm, diag_hbm,
     panel_out, super_out,
-    lists, table,
+    rows, cols, count, panel_rows, low, lists, table,
     blocks, lo0, lo1, lo2, acc0, acc1, acc2, new, diag,
-    rs_a, rs_b, rs_p, rs_m, u_all,
+    rs_a, rs_b, rs_p, rs_m, u_all, low_t, v_high, v_low,
     g0, g1, g2, c0, c1, c2, h0, h1, h2, p0, p1, p2, s0, s1, s2, y0, y1, y2, f0, f1, f2,
     local_sem, lo_send, lo_recv, rs_send, rs_recv, ar_send, ar_recv,
 ):
@@ -82,6 +82,16 @@
     block_copy = pltpu.make_async_copy(blocks_hbm.at[0], blocks.at[pl.ds(0, 96)], local_sem.at[0])
     new_copy = pltpu.make_async_copy(new_hbm, new, local_sem.at[1])
     diag_copy = pltpu.make_async_copy(diag_hbm, diag, local_sem.at[2])
+    low_copy = pltpu.make_async_copy(low_hbm, low, local_sem.at[4])
+    index_copies = [
+        pltpu.make_async_copy(src, dst, local_sem.at[5 + i])
+        for i, (src, dst) in enumerate(
+            ((rows_hbm, rows), (cols_hbm, cols), (count_hbm, count), (panel_hbm, panel_rows))
+        )
+    ]
+    low_copy.start()
+    for c in index_copies:
+        c.start()
     block_copy.start()
     new_copy.start()
     diag_copy.start()
@@ -231,48 +241,39 @@
             rs_copy(t, n).wait_recv()
         return (acc[t][:, quarter(0)] + (rs_p[t] + rs_m[t])).reshape(128, 256)
 
-    def low_rows(t):
-        return low[t, :, pl.ds(pl.multiple_of(z * 64, 64), 64), :].reshape(128, 256)
-
     def across(left, right):
         return lax.dot_general(left, right, (((0,), (0,)), ((), ())), preferred_element_type=F32)
 
     g = (g0, g1, g2)
 
-    def earlier(t):
-        total = jnp.dot(u_all[0], new[t, 0], preferred_element_type=F32)
-        for e in range(1, t):
-            total = total + jnp.dot(u_all[e], new[t, e], preferred_element_type=F32)
-        return total
-
     def panel(t):
         running = rs_third(t)
-        if t > 0:
-            running = running + earlier(t)
+        for e in range(t):
+            running = running + jnp.dot(u_all[e], new[t, e], preferred_element_type=F32)
         current = (-running).astype(BF16)
         u_all[t] = current
         panel_out[t] = current.reshape(2, 64, 256)
-        if t == 0:
-            g0[0] = across(current, low_rows(1))
-            g0[1] = across(current, low_rows(2))
-            g0[2] = across(low_rows(0), current)
-        elif t == 1:
-            g1[0] = across(current, low_rows(2))
-            g1[1] = across(low_rows(1), current)
 
     def halves(value):
         high = value.astype(BF16)
         return high, (value - high.astype(F32)).astype(BF16)
 
-    def last_contraction():
-        total = None
-        for part in halves(earlier(2)):
-            term = across(low_rows(2), part)
-            total = term if total is None else total + term
+    def turn_low():
+        for t in range(3):
+            low_t[t] = low[t].reshape(512, 256).T
+
+    def contract(t):
         for p in range(2):
-            for part in halves(acc2[p]):
-                total = total + across(low[2, p], part)
-        g2[0] = -total
+            rows_p = pl.ds(256 * p, 256)
+            value = acc[t][p]
+            for e in range(t):
+                for part in (v_low, v_high):
+                    value = value + jnp.dot(part[e, rows_p], new[t, e], preferred_element_type=F32)
+            v_high[t, rows_p], v_low[t, rows_p] = halves(-value)
+        for i, other in enumerate({0: (1, 2, 0), 1: (2, 1), 2: (2,)}[t]):
+            g[t][i] = jnp.dot(low_t[other], v_low[t], preferred_element_type=F32) + jnp.dot(
+                low_t[other], v_high[t], preferred_element_type=F32
+            )
 
     def ar(b, phase):
         gb, cb, hb, pb, sb, yb, fb = (
@@ -354,6 +355,7 @@
             total = term if total is None else total + term
         return total
 
+    low_copy.wait()
     pl.semaphore_wait(barrier, len(partners))
 
     @pl.when(is_src & (k == src_k))
@@ -375,11 +377,15 @@
                 arrived(t, own + s)
 
     gather_steps(((0, 1), (1, 1), (2, 1)), ())
+    for c in index_copies:
+        c.wait()
     found = slot_lists(rows[...], cols[...], count[0, 0], panel_rows, row, z)
     for i in range(3):
         lists[i : i + 1, :] = found[i]
     table_copy = pltpu.make_async_copy(lists, table, local_sem.at[3])
     table_copy.start()
+    turn_low()
+    new_copy.wait()
     gather_steps(((0, 2),), ((0, 1),))
     gather_steps(((1, 2), (0, 3)), ((1, 1),))
     gather_steps(((2, 2), (1, 3), (0, 4)), ((2, 1), (0, 2), (0, 3)))
@@ -388,63 +394,58 @@
     from_sibling(0)
     table_copy.wait()
     block_copy.wait()
-    multiply(0, 0, 10)
-    gather_steps(((2, 4),), ((2, 2), (2, 3)))
-    multiply(0, 10, 25)
+    multiply(0, 0, 25)
     rs_first(0)
-    gather_steps(((1, 5), (1, 6)), ())
+    contract(0)
+    ar(0, 0)
+    gather_steps(((2, 4), (1, 5), (1, 6)), ((2, 2),))
     from_sibling(1)
-    multiply(1, 0, 10)
+    ar(0, 1)
+    multiply(1, 0, 15)
+    gather_steps((), ((2, 3),))
+    multiply(1, 15, 25)
+    rs_first(1)
+    contract(1)
+    ar(1, 0)
+    gather_steps(((2, 5), (2, 6)), ())
     rs_second(0)
-    gather_steps(((2, 5), (2, 6)), ())
-    multiply(1, 10, 25)
-    rs_first(1)
-    new_copy.wait()
+    ar(0, 2)
+    ar(1, 1)
+    from_sibling(2)
+    multiply(2, 0, 25)
+    rs_first(2)
+    contract(2)
+    ar(2, 0)
+    ar(0, 3)
+    ar(2, 1)
+    rs_second(1)
+    ar(1, 2)
     panel(0)
-    ar(0, 0)
-    from_sibling(2)
-    multiply(2, 0, 10)
-    rs_second(1)
-    ar(0, 1)
-    multiply(2, 10, 25)
-    rs_first(2)
+    rs_second(2)
+    ar(2, 2)
+    ar(1, 3)
+    ar(0, 4)
     panel(1)
-    ar(1, 0)
-    last_contraction()
-    ar(2, 0)
-    ar(1, 1)
-    ar(2, 1)
-    rs_second(2)
-    ar(0, 2)
-    panel(2)
-    ar(1, 2)
-    ar(2, 2)
-    ar(0, 3)
-    ar(1, 3)
     ar(2, 3)
-    ar(0, 4)
     ar(0, 5)
     diag_copy.wait()
     y00 = diag[0] - f0[2]
-    y10 = -(f0[0] + times(y00, new[1, 0]))
-    super_out[0, 0] = y00
-    super_out[1, 0] = y10
+    y10 = -(f0[0].T + times(y00, new[1, 0]))
+    super_out[0] = y00
+    super_out[1] = y10
     ar(1, 4)
-    nothing = jnp.zeros((256, 256), F32)
-    super_out[0, 1] = nothing
-    super_out[0, 2] = nothing
-    super_out[1, 2] = nothing
-    y20 = -(f0[1] + (times(y00, new[2, 0]) + times(y10, new[2, 1])))
-    super_out[2, 0] = y20
+    y20 = -(f0[1].T + (times(y00, new[2, 0]) + times(y10, new[2, 1])))
+    super_out[3] = y20
     ar(2, 4)
     ar(1, 5)
+    panel(2)
     y11 = (diag[1] - f1[1]) - times(y10, new[1, 0], True)
-    super_out[1, 1] = y11
-    y21 = -(f1[0] + (times(y10.T, new[2, 0]) + times(y11, new[2, 1])))
-    super_out[2, 1] = y21
+    super_out[2] = y11
+    y21 = -(f1[0].T + (times(y10.T, new[2, 0]) + times(y11, new[2, 1])))
+    super_out[4] = y21
     rest = diag[2] - (times(y20, new[2, 0], True) + times(y21, new[2, 1], True))
     ar(2, 5)
-    super_out[2, 2] = rest - f2[0]
+    super_out[5] = rest - f2[0]
 
     for t in range(3):
         for n in range(6):
@@ -471,6 +472,12 @@
     def _():
         for t, n in sent["mid"]:
             send_done(t, n)
+
+
+def place_kernel(found, out):
+    for i in range(3):
+        for j in range(3):
+            out[i, j] = found[i * (i + 1) // 2 + j] if j <= i else jnp.zeros((256, 256), F32)
 
 
 def per_device(
@@ -483,22 +490,26 @@
     lower_new,
     diag_inverse,
 ):
-    smem = pl.BlockSpec(memory_space=pltpu.SMEM)
     vmem = pl.BlockSpec(memory_space=pltpu.VMEM)
     hbm = pl.BlockSpec(memory_space=pltpu.HBM)
 
     def each(*shape):
         return [pltpu.VMEM(tuple(nb if s is None else s for s in shape), F32) for nb in BUNDLES]
 
-    return pl.pallas_call(
+    panels, found = pl.pallas_call(
         kernel,
         out_shape=(
             jax.ShapeDtypeStruct((3, 2, 64, 256), BF16),
-            jax.ShapeDtypeStruct((3, 3, 256, 256), F32),
+            jax.ShapeDtypeStruct((6, 256, 256), F32),
         ),
-        in_specs=[vmem, vmem, smem, smem, vmem, hbm, hbm, hbm],
+        in_specs=[hbm] * 8,
         out_specs=(vmem, vmem),
         scratch_shapes=[
+            pltpu.VMEM((1, 96), jnp.int32),
+            pltpu.VMEM((1, 96), jnp.int32),
+            pltpu.SMEM((1, 1), jnp.int32),
+            pltpu.SMEM((64,), jnp.int32),
+            pltpu.VMEM((3, 2, 256, 256), BF16),
             pltpu.VMEM((3, 128), jnp.int32),
             pltpu.SMEM((3, 128), jnp.int32),
             pltpu.VMEM((97, 256, 256), BF16),
@@ -511,6 +522,9 @@
             pltpu.VMEM((3, 2, 64, 256), F32),
             pltpu.VMEM((3, 2, 64, 256), F32),
             pltpu.VMEM((3, 128, 256), BF16),
+            pltpu.VMEM((3, 256, 512), BF16),
+            pltpu.VMEM((3, 512, 256), BF16),
+            pltpu.VMEM((3, 512, 256), BF16),
             *each(None, 256, 256),
             *each(None, 128, 256),
             *each(None, 128, 256),
@@ -518,7 +532,7 @@
             *each(None, 8, 256),
             *each(4, None, 8, 256),
             *each(None, 256, 256),
-            pltpu.SemaphoreType.DMA((4,)),
+            pltpu.SemaphoreType.DMA((9,)),
             pltpu.SemaphoreType.DMA((3, 32)),
             pltpu.SemaphoreType.DMA((3, 16)),
             pltpu.SemaphoreType.DMA((3, 6)),
@@ -527,9 +541,16 @@
             pltpu.SemaphoreType.DMA((3, 7)),
         ],
         compiler_params=pltpu.CompilerParams(
-            collective_id=0, has_side_effects=True, vmem_limit_bytes=52 * 2**20
+            collective_id=0, has_side_effects=True, vmem_limit_bytes=60 * 2**20
         ),
     )(inverse_rows, inverse_cols, inverse_count, panel_rows, lower_old, inverse_blocks, lower_new, diag_inverse)
+    placed = pl.pallas_call(
+        place_kernel,
+        out_shape=jax.ShapeDtypeStruct((3, 3, 256, 256), F32),
+        in_specs=[vmem],
+        out_specs=vmem,
+    )(found)
+    return panels, placed
 
 
 def solution(mesh):

time: 88.6 us -> 81.9 us (0.924)
  local copies, waits for them, and re-layouts: 8.12 us -> 0.68 us
  Pallas kernels: 78.9 us -> 79.8 us
    unnamed x12 -> x3, local copies, waits for them, and re-layouts: 8.12 us -> 0.68 us
    pallas_call x0 -> x1, Pallas kernels: none -> 3 us  [per_device(): pl.pallas_call(place_kernel, out_shape=jax.ShapeDtypeStruct((3, 3, 256, 2...]
    pallas_call x1, Pallas kernels: 78.9 us -> 76.8 us  [per_device(): pl.pallas_call(kernel, out_shape=(jax.ShapeDtypeStruct((3, 2, 64, 256), B...]
where the time goes in v3:
time: 81.9 us; the launch traced here: 81.8 us
  Pallas kernels  79.8 us (97%)
  between operations  1.29 us (2%)
    pallas_call x1, Pallas kernels, per_device(): pl.pallas_call(kernel, out_shape=(jax.ShapeDtypeStruct((3, 2, 64, 256), B...  76.8 us
    pallas_call x1, Pallas kernels, per_device(): pl.pallas_call(place_kernel, out_shape=jax.ShapeDtypeStruct((3, 3, 256, 2...  3 us

profile of v3, /device:TPU:1, one launch (start us, length us, event | category | flops | bytes accessed | tf_op | source)
XLA Modules:
  0.0 81.8 jit_solution(7337282200908849394)
XLA Ops:
  1.3 76.8 %shard_map.95 = (bf16[3,2,64,256]{3,2,1,0:T(8,128)(2,1)}, f32[6,256,256]{2,1,0:T(8,128)}) custom-call(s32[1,96]{1,0:T(1,128)} %rows_hbm.1, s32[1,96]{1,0:T(1,128)} %cols_hbm.1, s32[1,1]{1,0:T(1,128)S(6)} %copy.11.count_hbm, s32[64]{0:T(128)} %panel_hbm.1, bf16[3,2,256,256]{3,2,1,0:T(8,128)(2,1)} %low_hbm.1, bf16[1,96,256,256]{3,2,1,0:T(8,128)(2,1)} %blocks_hbm.1, ...), custom_call_target="tpu_custom_call" | custom-call | tf_op jit(solution)/shard_map/pallas_call | solution.py:499
  78.1 0.0 copy-start
  78.1 3.0 %shard_map.96 = f32[3,3,256,256]{3,2,1,0:T(8,128)} custom-call(f32[6,256,256]{2,1,0:T(8,128)} %get-tuple-element.5.found), custom_call_target="tpu_custom_call" | custom-call | tf_op jit(solution)/shard_map/pallas_call | solution.py:547
  81.1 0.0 copy-done
  81.1 0.7 copy.12
Async XLA Ops:
  78.1 3.0 %copy-start = (bf16[3,2,64,256]{3,2,1,0:T(8,128)(2,1)S(1)}, bf16[3,2,64,256]{3,2,1,0:T(8,128)(2,1)}, u32[]{:S(2)}) copy-start(bf16[3,2,64,256]{3,2,1,0:T(8,128)(2,1)} %get-tuple-element.8) | copy-start | bytes 589828

commit v4 on v3

--- a/solution.py
+++ b/solution.py
@@ -394,20 +394,23 @@
     from_sibling(0)
     table_copy.wait()
     block_copy.wait()
-    multiply(0, 0, 25)
+    multiply(0, 0, 15)
+    gather_steps(((2, 4), (1, 5)), ((2, 2),))
+    multiply(0, 15, 25)
     rs_first(0)
     contract(0)
     ar(0, 0)
-    gather_steps(((2, 4), (1, 5), (1, 6)), ((2, 2),))
+    gather_steps(((1, 6),), ())
     from_sibling(1)
     ar(0, 1)
+    gather_steps((), ((2, 3),))
     multiply(1, 0, 15)
-    gather_steps((), ((2, 3),))
+    gather_steps(((2, 5),), ())
     multiply(1, 15, 25)
+    gather_steps(((2, 6),), ())
     rs_first(1)
     contract(1)
     ar(1, 0)
-    gather_steps(((2, 5), (2, 6)), ())
     rs_second(0)
     ar(0, 2)
     ar(1, 1)
@@ -433,24 +436,11 @@
     y10 = -(f0[0].T + times(y00, new[1, 0]))
     super_out[0] = y00
     super_out[1] = y10
-    ar(1, 4)
     y20 = -(f0[1].T + (times(y00, new[2, 0]) + times(y10, new[2, 1])))
     super_out[3] = y20
-    ar(2, 4)
-    ar(1, 5)
-    panel(2)
-    y11 = (diag[1] - f1[1]) - times(y10, new[1, 0], True)
-    super_out[2] = y11
-    y21 = -(f1[0].T + (times(y10.T, new[2, 0]) + times(y11, new[2, 1])))
-    super_out[4] = y21
-    rest = diag[2] - (times(y20, new[2, 0], True) + times(y21, new[2, 1], True))
-    ar(2, 5)
-    super_out[5] = rest - f2[0]
-
-    for t in range(3):
-        for n in range(6):
-            rs_copy(t, n).wait_send()
-
+    super_out[2] = diag[1] - times(y10, new[1, 0], True)
+    super_out[4] = times(y10.T, new[2, 0])
+    super_out[5] = diag[2] - times(y20, new[2, 0], True)
     def send_done(t, n):
         pltpu.make_async_remote_copy(
             lo[t].at[0], lo[t].at[0], lo_send.at[t, n], lo_recv.at[t, 0],
@@ -472,6 +462,21 @@
     def _():
         for t, n in sent["mid"]:
             send_done(t, n)
+
+    ar(1, 4)
+    ar(2, 4)
+    panel(2)
+    ar(1, 5)
+    y11 = super_out[2] - f1[1]
+    super_out[2] = y11
+    y21 = -(f1[0].T + (super_out[4] + times(y11, new[2, 1])))
+    super_out[4] = y21
+    rest = super_out[5] - times(y21, new[2, 1], True)
+    for t in range(3):
+        for n in range(6):
+            rs_copy(t, n).wait_send()
+    ar(2, 5)
+    super_out[5] = rest - f2[0]
 
 
 def place_kernel(found, out):

time: 81.9 us -> 80.9 us (0.988)
  Pallas kernels: 79.8 us -> 78.8 us
    pallas_call x1, Pallas kernels: 76.8 us -> 75.8 us  [per_device(): pl.pallas_call(kernel, out_shape=(jax.ShapeDtypeStruct((3, 2, 64, 256), B...]
where the time goes in v4:
time: 80.9 us; the launch traced here: 80.8 us
  Pallas kernels  78.8 us (97%)
  between operations  1.29 us (2%)
    pallas_call x1, Pallas kernels, per_device(): pl.pallas_call(kernel, out_shape=(jax.ShapeDtypeStruct((3, 2, 64, 256), B...  75.8 us
    pallas_call x1, Pallas kernels, per_device(): pl.pallas_call(place_kernel, out_shape=jax.ShapeDtypeStruct((3, 3, 256, 2...  3 us

profile of v4, /device:TPU:1, one launch (start us, length us, event | category | flops | bytes accessed | tf_op | source)
XLA Modules:
  0.0 80.8 jit_solution(4105142210437876758)
XLA Ops:
  1.3 75.8 %shard_map.95 = (bf16[3,2,64,256]{3,2,1,0:T(8,128)(2,1)}, f32[6,256,256]{2,1,0:T(8,128)}) custom-call(s32[1,96]{1,0:T(1,128)} %rows_hbm.1, s32[1,96]{1,0:T(1,128)} %cols_hbm.1, s32[1,1]{1,0:T(1,128)S(6)} %copy.11.count_hbm, s32[64]{0:T(128)} %panel_hbm.1, bf16[3,2,256,256]{3,2,1,0:T(8,128)(2,1)} %low_hbm.1, bf16[1,96,256,256]{3,2,1,0:T(8,128)(2,1)} %blocks_hbm.1, ...), custom_call_target="tpu_custom_call" | custom-call | tf_op jit(solution)/shard_map/pallas_call | solution.py:504
  77.1 0.0 copy-start
  77.1 3.0 %shard_map.96 = f32[3,3,256,256]{3,2,1,0:T(8,128)} custom-call(f32[6,256,256]{2,1,0:T(8,128)} %get-tuple-element.5.found), custom_call_target="tpu_custom_call" | custom-call | tf_op jit(solution)/shard_map/pallas_call | solution.py:552
  80.1 0.0 copy-done
  80.1 0.7 copy.12
Async XLA Ops:
  77.1 3.0 %copy-start = (bf16[3,2,64,256]{3,2,1,0:T(8,128)(2,1)S(1)}, bf16[3,2,64,256]{3,2,1,0:T(8,128)(2,1)}, u32[]{:S(2)}) copy-start(bf16[3,2,64,256]{3,2,1,0:T(8,128)(2,1)} %get-tuple-element.8) | copy-start | bytes 589828

commit v5 on v4

--- a/solution.py
+++ b/solution.py
@@ -8,11 +8,12 @@
 from jax.sharding import PartitionSpec as P
 
 MESH = pl.DeviceIdType.MESH
+F32 = jnp.float32
+BF16 = jnp.bfloat16
 GROUP = 4
 BUNDLES = (3, 2, 1)
+KINDS = (BF16, BF16, BF16)
 PLANE = tuple((dx, dy) for dy in (1, 3, 0, 2) for dx in (1, 3, 0, 2) if (dx, dy) != (0, 0))
-F32 = jnp.float32
-BF16 = jnp.bfloat16
 
 
 def slot_lists(rows, cols, count, panel_rows, row, col):
@@ -291,7 +292,7 @@
             )
 
         mine = y * 4 + x
-        base = 128 * k + 8 * mine
+        base = 16 * k + mine
         peers = [(dx, dy) for dx, dy in PLANE]
 
         def core():
@@ -301,25 +302,25 @@
             copies = []
             for dx, dy in peers:
                 other = (y + dy) % 4 * 4 + (x + dx) % 4
-                copies.append(copy(1, hb.at[:, ds(8 * other, 8)], pb.at[mine], at(dx=dx, dy=dy)))
+                copies.append(copy(1, hb.at[:, other], pb.at[mine], at(dx=dx, dy=dy)))
             return copies
 
         def over_z():
             return [copy(1 + d, sb, yb.at[z], at(dz=d)) for d in (1, 3, 2)]
 
         def back_plane():
-            part = fb.at[:, ds(base, 8)]
+            part = fb.at[:, base]
             return [copy(5, part, part, at(dx=dx, dy=dy)) for dx, dy in peers]
 
         def back_core():
-            part = fb.at[:, ds(128 * k, 128)]
+            part = fb.at[:, ds(16 * k, 16)]
             return [copy(6, part, part, sib)]
 
         def plane_wait():
-            return [copy(1, hb.at[:, pl.ds(0, 120)], hb.at[:, pl.ds(0, 120)], sib)]
+            return [copy(1, hb.at[:, pl.ds(0, 15)], hb.at[:, pl.ds(0, 15)], sib)]
 
         def back_wait():
-            return [copy(5, fb.at[:, pl.ds(0, 120)], fb.at[:, pl.ds(0, 120)], sib)]
+            return [copy(5, fb.at[:, pl.ds(0, 15)], fb.at[:, pl.ds(0, 15)], sib)]
 
         stages = (core, over_plane, over_z, back_plane, back_core)
         waits = (core, plane_wait, over_z, back_wait, back_core)
@@ -327,16 +328,17 @@
             for c in waits[phase - 1]():
                 c.wait_recv()
         if phase == 1:
-            hb[...] = gb[:, ds(128 * k, 128)] + cb[...]
-            pb[mine] = hb[:, ds(8 * mine, 8)]
+            half = gb[:, ds(128 * k, 128)] + cb[...]
+            hb[...] = half.reshape(hb.shape).astype(hb.dtype)
+            pb[mine] = hb[:, mine]
         if phase == 2:
-            total = [pb[i] for i in range(16)]
+            total = [pb[i].astype(F32) for i in range(16)]
             while len(total) > 1:
                 total = [total[i] + total[i + 1] for i in range(0, len(total), 2)]
             sb[...] = total[0]
             yb[z] = total[0]
         if phase == 3:
-            fb[:, ds(base, 8)] = (yb[0] + yb[1]) + (yb[2] + yb[3])
+            fb[:, base] = ((yb[0] + yb[1]) + (yb[2] + yb[3])).astype(fb.dtype)
         if phase < 5:
             for c in stages[phase]():
                 c.start()
@@ -354,6 +356,9 @@
                 term = jnp.dot(part, factor, preferred_element_type=F32)
             total = term if total is None else total + term
         return total
+
+    def summed(f, i):
+        return f[i].reshape(256, 256).astype(F32)
 
     low_copy.wait()
     pl.semaphore_wait(barrier, len(partners))
@@ -432,11 +437,11 @@
     ar(2, 3)
     ar(0, 5)
     diag_copy.wait()
-    y00 = diag[0] - f0[2]
-    y10 = -(f0[0].T + times(y00, new[1, 0]))
+    y00 = diag[0] - summed(f0, 2)
+    y10 = -(summed(f0, 0).T + times(y00, new[1, 0]))
     super_out[0] = y00
     super_out[1] = y10
-    y20 = -(f0[1].T + (times(y00, new[2, 0]) + times(y10, new[2, 1])))
+    y20 = -(summed(f0, 1).T + (times(y00, new[2, 0]) + times(y10, new[2, 1])))
     super_out[3] = y20
     super_out[2] = diag[1] - times(y10, new[1, 0], True)
     super_out[4] = times(y10.T, new[2, 0])
@@ -467,16 +472,16 @@
     ar(2, 4)
     panel(2)
     ar(1, 5)
-    y11 = super_out[2] - f1[1]
+    y11 = super_out[2] - summed(f1, 1)
     super_out[2] = y11
-    y21 = -(f1[0].T + (super_out[4] + times(y11, new[2, 1])))
+    y21 = -(summed(f1, 0).T + (super_out[4] + times(y11, new[2, 1])))
     super_out[4] = y21
     rest = super_out[5] - times(y21, new[2, 1], True)
     for t in range(3):
         for n in range(6):
             rs_copy(t, n).wait_send()
     ar(2, 5)
-    super_out[5] = rest - f2[0]
+    super_out[5] = rest - summed(f2, 0)
 
 
 def place_kernel(found, out):
@@ -497,6 +502,11 @@
 ):
     vmem = pl.BlockSpec(memory_space=pltpu.VMEM)
     hbm = pl.BlockSpec(memory_space=pltpu.HBM)
+
+    def sent(*shape):
+        return [
+            pltpu.VMEM(tuple(nb if s is None else s for s in shape), kind) for nb, kind in zip(BUNDLES, KINDS)
+        ]
 
     def each(*shape):
         return [pltpu.VMEM(tuple(nb if s is None else s for s in shape), F32) for nb in BUNDLES]
@@ -532,11 +542,11 @@
             pltpu.VMEM((3, 512, 256), BF16),
             *each(None, 256, 256),
             *each(None, 128, 256),
-            *each(None, 128, 256),
-            *each(16, None, 8, 256),
+            *sent(None, 16, 8, 256),
+            *sent(16, None, 8, 256),
             *each(None, 8, 256),
             *each(4, None, 8, 256),
-            *each(None, 256, 256),
+            *sent(None, 32, 8, 256),
             pltpu.SemaphoreType.DMA((9,)),
             pltpu.SemaphoreType.DMA((3, 32)),
             pltpu.SemaphoreType.DMA((3, 16)),

time: 80.9 us -> 76.7 us (0.948)
  Pallas kernels: 78.8 us -> 74.6 us
    pallas_call x1, Pallas kernels: 75.8 us -> 71.6 us  [per_device(): pl.pallas_call(kernel, out_shape=(jax.ShapeDtypeStruct((3, 2, 64, 256), B...]
where the time goes in v5:
time: 76.7 us; the launch traced here: 76.6 us
  Pallas kernels  74.6 us (97%)
  between operations  1.29 us (2%)
    pallas_call x1, Pallas kernels, per_device(): pl.pallas_call(kernel, out_shape=(jax.ShapeDtypeStruct((3, 2, 64, 256), B...  71.6 us
    pallas_call x1, Pallas kernels, per_device(): pl.pallas_call(place_kernel, out_shape=jax.ShapeDtypeStruct((3, 3, 256, 2...  3 us

profile of v5, /device:TPU:1, one launch (start us, length us, event | category | flops | bytes accessed | tf_op | source)
XLA Modules:
  0.0 76.6 jit_solution(10992951351700612880)
XLA Ops:
  1.3 71.6 %shard_map.95 = (bf16[3,2,64,256]{3,2,1,0:T(8,128)(2,1)}, f32[6,256,256]{2,1,0:T(8,128)}) custom-call(s32[1,96]{1,0:T(1,128)} %rows_hbm.1, s32[1,96]{1,0:T(1,128)} %cols_hbm.1, s32[1,1]{1,0:T(1,128)S(6)} %copy.11.count_hbm, s32[64]{0:T(128)} %panel_hbm.1, bf16[3,2,256,256]{3,2,1,0:T(8,128)(2,1)} %low_hbm.1, bf16[1,96,256,256]{3,2,1,0:T(8,128)(2,1)} %blocks_hbm.1, ...), custom_call_target="tpu_custom_call" | custom-call | tf_op jit(solution)/shard_map/pallas_call | solution.py:514
  72.9 0.0 copy-start
  72.9 3.0 %shard_map.96 = f32[3,3,256,256]{3,2,1,0:T(8,128)} custom-call(f32[6,256,256]{2,1,0:T(8,128)} %get-tuple-element.5.found), custom_call_target="tpu_custom_call" | custom-call | tf_op jit(solution)/shard_map/pallas_call | solution.py:562
  75.9 0.0 copy-done
  75.9 0.7 copy.12
Async XLA Ops:
  72.9 3.0 %copy-start = (bf16[3,2,64,256]{3,2,1,0:T(8,128)(2,1)S(1)}, bf16[3,2,64,256]{3,2,1,0:T(8,128)(2,1)}, u32[]{:S(2)}) copy-start(bf16[3,2,64,256]{3,2,1,0:T(8,128)(2,1)} %get-tuple-element.8) | copy-start | bytes 589828

commit v6 on v5

--- a/solution.py
+++ b/solution.py
@@ -206,7 +206,7 @@
             acc[t][1] += product * (1.0 - weight)
             return carry
 
-        lax.fori_loop(begin, end, body, 0, unroll=5)
+        lax.fori_loop(begin, end, body, 0, unroll=25 if t == 2 else 5)
 
     def quarter(d):
         return pl.ds(pl.multiple_of((z + d) % 4 * 64, 64), 64)

time: 76.7 us -> 76.2 us (level)
  no operation moved by 1% of the time
where the time goes in v6:
time: 76.2 us; the launch traced here: 76 us
  Pallas kernels  74 us (97%)
  between operations  1.29 us (2%)
    pallas_call x1, Pallas kernels, per_device(): pl.pallas_call(kernel, out_shape=(jax.ShapeDtypeStruct((3, 2, 64, 256), B...  71 us
    pallas_call x1, Pallas kernels, per_device(): pl.pallas_call(place_kernel, out_shape=jax.ShapeDtypeStruct((3, 3, 256, 2...  3 us

profile of v6, /device:TPU:1, one launch (start us, length us, event | category | flops | bytes accessed | tf_op | source)
XLA Modules:
  0.0 76.0 jit_solution(4613703625940729639)
XLA Ops:
  1.3 71.0 %shard_map.95 = (bf16[3,2,64,256]{3,2,1,0:T(8,128)(2,1)}, f32[6,256,256]{2,1,0:T(8,128)}) custom-call(s32[1,96]{1,0:T(1,128)} %rows_hbm.1, s32[1,96]{1,0:T(1,128)} %cols_hbm.1, s32[1,1]{1,0:T(1,128)S(6)} %copy.11.count_hbm, s32[64]{0:T(128)} %panel_hbm.1, bf16[3,2,256,256]{3,2,1,0:T(8,128)(2,1)} %low_hbm.1, bf16[1,96,256,256]{3,2,1,0:T(8,128)(2,1)} %blocks_hbm.1, ...), custom_call_target="tpu_custom_call" | custom-call | tf_op jit(solution)/shard_map/pallas_call | solution.py:514
  72.3 0.0 copy-start
  72.3 3.0 %shard_map.96 = f32[3,3,256,256]{3,2,1,0:T(8,128)} custom-call(f32[6,256,256]{2,1,0:T(8,128)} %get-tuple-element.5.found), custom_call_target="tpu_custom_call" | custom-call | tf_op jit(solution)/shard_map/pallas_call | solution.py:562
  75.3 0.0 copy-done
  75.3 0.7 copy.12
Async XLA Ops:
  72.3 3.0 %copy-start = (bf16[3,2,64,256]{3,2,1,0:T(8,128)(2,1)S(1)}, bf16[3,2,64,256]{3,2,1,0:T(8,128)(2,1)}, u32[]{:S(2)}) copy-start(bf16[3,2,64,256]{3,2,1,0:T(8,128)(2,1)} %get-tuple-element.8) | copy-start | bytes 589828
